TPU v7x, 1024 devices: a whole 4x8x16 slice. The times are simulated.
1024 devices in a mesh: clus: 16 (over y, core), sub: 64 (over z, x).
Axes of the slice: x: 4, y: 8, z: 16, core: 2. Of those that a mesh axis runs over, the one named last changes fastest.
Arguments:
- dual_ops: bfloat16 [1024, 1024, 1024], P(('clus', 'sub')), as said below
- dual_rhs: bfloat16 [1024, 1024, 128], P(('clus', 'sub')), as said below
- partner: int32 [1024, 28], P(('clus', 'sub')), may hold values from -1 to 1791, as said below
- cluster_basis: bfloat16 [1024, 192, 896], P(('clus', 'sub')), as said below
- global_basis: bfloat16 [1024, 6, 896], P(('clus', 'sub')), as said below
- cluster_inverse: float32 [16, 192, 192], P('clus'), as said below
- global_inverse: float32 [96, 96], replicated, as said below
Outputs:
- multipliers: float32 [1024, 1024, 128], P(('clus', 'sub'))
Inputs may be any that keep to these rules, and one draw needn't show every extreme that they name: partner[s, b] is -1 or a value g naming block g % 28 of subdomain (s // 64) * 64 + g // 28, another subdomain of the same cluster, whose entry for that block names block b of s back; two subdomains share at most 1 glued blocks, and some two share exactly 1. Each dual_ops[s] is symmetric positive definite. `dual_rhs`: the copies of a multiplier agree: on every row where weight is 1/2 the row equals the same row of the partner copy. `cluster_basis`: on every interface row glued to a partner block the modes equal those of the partner row. `global_basis`: on every interface row glued to a partner block the modes equal those of the partner row. Each cluster_inverse[c] is symmetric positive definite. global_inverse is symmetric positive definite.
All inputs are finite; a program needn't handle non-finite values.
Results may differ from a plain program's by a relative error of at most 0.001.
Values sent between devices are 32-bit elements; how exact they have to be, the bound alone decides.
No kernel may reach another device: no remote copies, remote signals or barrier semaphores. Data moves between devices by JAX's collectives and lax.ppermute only.
A program may use at most 32 MiB of HBM per device.

v0:
```python
import jax
import jax.numpy as jnp
from jax import lax
from jax.sharding import PartitionSpec as P

FACE = 64
BLK = 32
MODES = 6
ITERS = 3
NIB = 28


PRECISE = lax.Precision.HIGHEST


def with_halo(block, sides, width):
    for axis, dim in sides:
        count = lax.axis_size(axis)
        forward = [(i, i + 1) for i in range(count - 1)]
        backward = [(target, source) for source, target in forward]
        low = lax.ppermute(
            lax.slice_in_dim(block, block.shape[dim] - width, None, axis=dim), axis, forward
        )
        high = lax.ppermute(lax.slice_in_dim(block, 0, width, axis=dim), axis, backward)
        block = jnp.concatenate([low, block, high], axis=dim)
    return block


def cluster_sum(values):
    return lax.psum(values, "sub")


def global_sum(values):
    return lax.psum(values, "clus")


def global_gather(values):
    return lax.all_gather(values, "clus", axis=0, tiled=True)


def block_plan(partner_ids):
    sub_count = lax.axis_size("sub")
    capacity = (NIB + sub_count - 1) // sub_count
    linked = partner_ids >= 0
    target = jnp.where(linked, partner_ids // NIB, -1)
    shared = (target[:, None] == target[None, :]) & linked[:, None] & linked[None, :]
    block_ids = jnp.arange(NIB)
    send_rank = jnp.sum(shared & (block_ids[None, :] < block_ids[:, None]), axis=1)
    recv_rank = jnp.sum(shared & (partner_ids[None, :] < partner_ids[:, None]), axis=1)
    send_slot = jnp.where(linked, target * capacity + send_rank, -1)
    slot_ids = jnp.arange(sub_count * capacity)
    chosen = send_slot[None, :] == slot_ids[:, None]
    source = jnp.sum(jnp.where(chosen, block_ids[None, :], 0), axis=1)
    filled = jnp.any(chosen, axis=1)
    recv_slot = jnp.where(linked, target * capacity + recv_rank, 0)
    return (linked, source, filled, recv_slot)


def swap_blocks(inner_values, plan):
    linked, source, filled, recv_slot = plan
    load_cases = inner_values.shape[1]
    blocks = inner_values.reshape(NIB, BLK, load_cases)
    outgoing = jnp.where(filled[:, None, None], jnp.take(blocks, source, axis=0), 0.0)
    incoming = lax.all_to_all(outgoing, "sub", split_axis=0, concat_axis=0, tiled=True)
    interior = jnp.where(linked[:, None, None], jnp.take(incoming, recv_slot, axis=0), 0.0)
    return interior.reshape(NIB * BLK, load_cases)


def face_copy(face_values):
    extended = with_halo(face_values, (("clus", 0),), FACE)
    return jnp.concatenate([extended[:FACE], extended[3 * FACE :]], axis=0)


def slot_weights(partner_ids):
    cluster = lax.axis_index("clus")
    cluster_count = lax.axis_size("clus")
    lower_face = jnp.where(cluster > 0, 0.5, 1.0).astype(jnp.float32) * jnp.ones(
        (FACE,), jnp.float32
    )
    upper_face = jnp.where(cluster < cluster_count - 1, 0.5, 1.0).astype(jnp.float32) * jnp.ones(
        (FACE,), jnp.float32
    )
    interior = jnp.repeat(jnp.where(partner_ids >= 0, 0.5, 1.0).astype(jnp.float32), BLK)
    return jnp.concatenate([lower_face, upper_face, interior])[:, None]


def coarse_parts(weighted, basis_cluster, basis_global):
    interior = weighted[2 * FACE :]
    return (
        jnp.dot(basis_cluster, interior, precision=PRECISE),
        jnp.dot(basis_global, interior, precision=PRECISE),
    )


def corrected(vector, cluster_amounts, global_amounts, basis_cluster, basis_global):
    contract = (((0,), (0,)), ((), ()))
    extra = lax.dot_general(basis_cluster, cluster_amounts, contract, precision=PRECISE)
    extra = extra + lax.dot_general(basis_global, global_amounts, contract, precision=PRECISE)
    return jnp.concatenate([vector[: 2 * FACE], vector[2 * FACE :] + extra], axis=0)


def on_device(
    dual_ops, dual_rhs, partner, cluster_basis, global_basis, cluster_inverse, global_inverse
):
    operator = dual_ops[0]
    partner_ids = partner[0]
    plan = block_plan(partner_ids)
    weight = slot_weights(partner_ids)
    basis_cluster = cluster_basis[0].astype(jnp.float32)
    basis_global = global_basis[0].astype(jnp.float32)
    inverse_cluster = cluster_inverse[0]
    cluster = lax.axis_index("clus")
    residual = dual_rhs[0].astype(jnp.float32)
    multipliers = jnp.zeros_like(residual)

    def own_rows(full):
        return lax.dynamic_slice_in_dim(full, cluster * MODES, MODES, 0)

    def weighted_dot(first, second):
        return jnp.sum(weight * first * second, axis=0)

    def precondition(cluster_proj, global_full, vector):
        cluster_amounts = jnp.dot(inverse_cluster, cluster_proj, precision=PRECISE)
        global_amounts = jnp.dot(global_inverse, global_full, precision=PRECISE)
        return corrected(
            vector, cluster_amounts, own_rows(global_amounts), basis_cluster, basis_global
        )

    def apply_coarse(vector):
        cluster_part, global_part = coarse_parts(weight * vector, basis_cluster, basis_global)
        cluster_proj, global_proj = cluster_sum((cluster_part, global_part))
        global_full = global_gather(global_proj)
        return precondition(cluster_proj, global_full, vector)

    def global_dot(first, second):
        return global_sum(cluster_sum(weighted_dot(first, second)))

    precond = apply_coarse(residual)
    energy_now = global_dot(residual, precond)
    direction = precond
    for iteration in range(ITERS):
        narrow = direction.astype(jnp.bfloat16)
        products = jnp.dot(operator, narrow, preferred_element_type=jnp.float32)
        interior = swap_blocks(products[2 * FACE :], plan)
        faces = face_copy(products[: 2 * FACE])
        products, applied = (products, products + jnp.concatenate([faces, interior], axis=0))
        step_size = energy_now / global_dot(direction, applied)
        multipliers = multipliers + step_size * direction
        residual = residual - step_size * applied
        precond = apply_coarse(residual)
        energy_next = global_dot(residual, precond)
        direction = precond + energy_next / energy_now * direction
        energy_now = energy_next
    return multipliers[None]


def solution(mesh):
    return jax.shard_map(
        on_device,
        mesh=mesh,
        in_specs=(
            P(("clus", "sub"), None, None),
            P(("clus", "sub"), None, None),
            P(("clus", "sub"), None),
            P(("clus", "sub"), None, None),
            P(("clus", "sub"), None, None),
            P("clus", None, None),
            P(),
        ),
        out_specs=P(("clus", "sub"), None, None),
        check_vma=False,
    )
```

profile of v0, /device:TPU:1, one launch (start us, length us, event | category | flops | bytes accessed | tf_op | source)
XLA Modules:
  0.0 2244.6 jit_solution(9507731529372440103)
XLA Ops:
  8.8 2.1 convolution_bitcast_fusion.2
  14.9 129.4 %psum.127 = f32[6,128]{1,0:T(8,128)S(1)} all-reduce(f32[6,128]{1,0:T(8,128)S(1)} %convolution_bitcast_fusion.5), channel_id=1, replica_groups=mesh['clus'=16,'sub'=64] {'sub'}, use_global_device_ids=true, to_apply=%region_1.2 | all-reduce | flops 768 | bytes 6144 | tf_op jit(solution)/shard_map/psum | solution.py:30
  144.4 46.1 %all-gather = f32[16,6,128]{2,1,0:T(8,128)S(1)} all-gather(f32[1,6,128]{2,1,0:T(8,128)S(1)} %bitcast.149), channel_id=1, replica_groups=mesh['clus'=16,'sub'=64] {'clus'}, dimensions={0}, use_global_device_ids=true | all-gather | bytes 52224 | tf_op jit(solution)/shard_map/all_gather | solution.py:38
  192.8 94.5 %all-reduce.6.cloned.1.call-done = f32[192,128]{1,0:T(8,128)} async-done(((f32[192,128]{1,0:T(8,128)}), f32[192,128]{1,0:T(8,128)}) %all-reduce.6.cloned.1.call-update) | async-done | bytes 98320 | tf_op jit(solution)/shard_map/psum | solution.py:30
  292.1 2.0 copy.27
  294.1 2.8 gather_fusion
  296.9 2.5 select_select_fusion.2
  299.4 9.9 all-to-all-start
  311.9 14.0 collective-permute-start
  325.9 1.9 collective-permute-start.1
  327.8 25.7 %all-to-all-done = f32[64,32,128]{2,1,0:T(8,128)} async-done(((f32[64,32,128]{2,1,0:T(8,128)}), f32[64,32,128]{2,1,0:T(8,128)}, u32[]{:S(2)}, u32[]{:S(2)}) %all-to-all-start) | async-done | bytes 1048608 | tf_op jit(solution)/shard_map/all_to_all | solution.py:64
  353.5 2.7 gather_fusion.1
  356.2 1.9 select_select_fusion.5
  358.2 2.0 copy.28
  360.1 2.0 multiply_reduce_fusion.3
  362.1 113.1 %all-reduce = (f32[128]{0:T(128)}, f32[128]{0:T(128)}) all-reduce(f32[128]{0:T(128)} %get-tuple-element.8, f32[128]{0:T(128)} %get-tuple-element.6), channel_id=1, replica_groups=mesh['clus'=16,'sub'=64] {'sub'}, use_global_device_ids=true, to_apply=%region_3.4 | all-reduce | flops 256 | bytes 2048 | tf_op jit(solution)/shard_map/psum | solution.py:30
  475.2 62.4 %all-reduce.1 = (f32[128]{0:T(128)}, f32[128]{0:T(128)}) all-reduce(f32[128]{0:T(128)} %get-tuple-element.11, f32[128]{0:T(128)} %get-tuple-element.12), channel_id=1, replica_groups=mesh['clus'=16,'sub'=64] {'clus'}, use_global_device_ids=true, to_apply=%region_4.5 | all-reduce | flops 256 | bytes 2048 | tf_op jit(solution)/shard_map/psum | solution.py:34
  538.3 2.1 broadcast_multiply_fusion.1
  542.5 111.2 %psum.133 = f32[6,128]{1,0:T(8,128)S(1)} all-reduce(f32[6,128]{1,0:T(8,128)} %convolution_bitcast_fusion.4), channel_id=1, replica_groups=mesh['clus'=16,'sub'=64] {'sub'}, use_global_device_ids=true, to_apply=%region_13.16 | all-reduce | flops 768 | bytes 6144 | tf_op jit(solution)/shard_map/psum | solution.py:30
  653.7 44.3 %all-gather.1 = f32[16,6,128]{2,1,0:T(8,128)} all-gather(f32[1,6,128]{2,1,0:T(8,128)S(1)} %bitcast.150), channel_id=1, replica_groups=mesh['clus'=16,'sub'=64] {'clus'}, dimensions={0}, use_global_device_ids=true | all-gather | bytes 52224 | tf_op jit(solution)/shard_map/all_gather | solution.py:38
  698.0 1.5 reshape.371
  699.5 1.6 fusion.74
  701.1 1.5 slice_bitcast_fusion.2
  702.6 258.0 %all-reduce.8.cloned.1.call-done = f32[192,128]{1,0:T(8,128)} async-done(((f32[192,128]{1,0:T(8,128)}), f32[192,128]{1,0:T(8,128)}) %all-reduce.8.cloned.1.call-update) | async-done | bytes 98320 | tf_op jit(solution)/shard_map/psum | solution.py:30
  962.3 1.5 fusion.18
  965.3 114.0 %psum.134 = f32[128]{0:T(128)S(1)} all-reduce(f32[128]{0:T(128)} %multiply_reduce_fusion.2), channel_id=1, replica_groups=mesh['clus'=16,'sub'=64] {'sub'}, use_global_device_ids=true, to_apply=%region_15.18 | all-reduce | flops 128 | bytes 1024 | tf_op jit(solution)/shard_map/psum | solution.py:30
  1079.3 60.8 %psum.135 = f32[128]{0:T(128)S(1)} all-reduce(f32[128]{0:T(128)S(1)} %psum.134), channel_id=1, replica_groups=mesh['clus'=16,'sub'=64] {'clus'}, use_global_device_ids=true, to_apply=%region_16.19 | all-reduce | flops 128 | bytes 1024 | tf_op jit(solution)/shard_map/psum | solution.py:34
  1145.5 2.0 copy.29
  1147.4 2.8 gather_fusion.2
  1150.2 2.5 select_select_fusion.1
  1152.7 9.0 all-to-all-start.1
  1161.7 1.6 fusion.71
  1163.4 1.9 collective-permute-start.2
  1165.3 2.4 collective-permute-start.3
  1167.7 45.4 %all-to-all-done.1 = f32[64,32,128]{2,1,0:T(8,128)} async-done(((f32[64,32,128]{2,1,0:T(8,128)}), f32[64,32,128]{2,1,0:T(8,128)}, u32[]{:S(2)}, u32[]{:S(2)}) %all-to-all-start.1) | async-done | bytes 1048608 | tf_op jit(solution)/shard_map/all_to_all | solution.py:64
  1213.1 2.7 gather_fusion.3
  1215.8 1.9 select_select_fusion.4
  1217.8 2.0 copy.30
  1221.2 113.4 %psum.136 = f32[128]{0:T(128)S(1)} all-reduce(f32[128]{0:T(128)S(1)} %multiply_reduce_fusion.1), channel_id=1, replica_groups=mesh['clus'=16,'sub'=64] {'sub'}, use_global_device_ids=true, to_apply=%region_18.21 | all-reduce | flops 128 | bytes 1024 | tf_op jit(solution)/shard_map/psum | solution.py:30
  1334.5 53.8 %psum.137 = f32[128]{0:T(128)S(1)} all-reduce(f32[128]{0:T(128)S(1)} %psum.136), channel_id=1, replica_groups=mesh['clus'=16,'sub'=64] {'clus'}, use_global_device_ids=true, to_apply=%region_19.22 | all-reduce | flops 128 | bytes 1024 | tf_op jit(solution)/shard_map/psum | solution.py:34
  1388.3 2.3 broadcast_multiply_fusion
  1392.6 111.1 %psum.139 = f32[6,128]{1,0:T(8,128)S(1)} all-reduce(f32[6,128]{1,0:T(8,128)S(1)} %convolution_bitcast_fusion.3), channel_id=1, replica_groups=mesh['clus'=16,'sub'=64] {'sub'}, use_global_device_ids=true, to_apply=%region_21.24 | all-reduce | flops 768 | bytes 6144 | tf_op jit(solution)/shard_map/psum | solution.py:30
  1503.6 44.3 %all-gather.2 = f32[16,6,128]{2,1,0:T(8,128)} all-gather(f32[1,6,128]{2,1,0:T(8,128)S(1)} %bitcast.151), channel_id=1, replica_groups=mesh['clus'=16,'sub'=64] {'clus'}, dimensions={0}, use_global_device_ids=true | all-gather | bytes 52224 | tf_op jit(solution)/shard_map/all_gather | solution.py:38
  1549.4 1.6 fusion.75
  1551.0 1.5 fusion.70
  1552.5 258.0 %all-reduce.10.cloned.1.call-done = f32[192,128]{1,0:T(8,128)} async-done(((f32[192,128]{1,0:T(8,128)}), f32[192,128]{1,0:T(8,128)}) %all-reduce.10.cloned.1.call-update) | async-done | bytes 98320 | tf_op jit(solution)/shard_map/psum | solution.py:30
  1812.3 1.5 fusion.16
  1814.7 114.0 %psum.140 = f32[128]{0:T(128)S(1)} all-reduce(f32[128]{0:T(128)S(1)} %multiply_reduce_fusion), channel_id=1, replica_groups=mesh['clus'=16,'sub'=64] {'sub'}, use_global_device_ids=true, to_apply=%region_23.26 | all-reduce | flops 128 | bytes 1024 | tf_op jit(solution)/shard_map/psum | solution.py:30
  1928.7 60.8 %psum.141 = f32[128]{0:T(128)S(1)} all-reduce(f32[128]{0:T(128)S(1)} %psum.140), channel_id=1, replica_groups=mesh['clus'=16,'sub'=64] {'clus'}, use_global_device_ids=true, to_apply=%region_24.27 | all-reduce | flops 128 | bytes 1024 | tf_op jit(solution)/shard_map/psum | solution.py:34
  1989.5 1.8 fusion.12
  1992.9 2.0 copy.31
  1994.9 2.8 gather_fusion.4
  1997.7 2.5 select_select_fusion
  2000.2 8.9 all-to-all-start.2
  2009.8 1.6 fusion.69
  2011.4 1.9 collective-permute-start.4
  2013.3 2.4 collective-permute-start.5
  2015.7 44.7 %all-to-all-done.2 = f32[64,32,128]{2,1,0:T(8,128)} async-done(((f32[64,32,128]{2,1,0:T(8,128)}), f32[64,32,128]{2,1,0:T(8,128)}, u32[]{:S(2)}, u32[]{:S(2)}) %all-to-all-start.2) | async-done | bytes 1048608 | tf_op jit(solution)/shard_map/all_to_all | solution.py:64
  2060.5 2.7 gather_fusion.5
  2063.2 2.0 select_select_fusion.3
  2065.1 2.0 copy.32
  2067.1 1.6 fusion.22
  2068.7 113.4 %psum.142 = f32[128]{0:T(128)S(1)} all-reduce(f32[128]{0:T(128)S(1)} %fusion.22), channel_id=1, replica_groups=mesh['clus'=16,'sub'=64] {'sub'}, use_global_device_ids=true, to_apply=%region_26.29 | all-reduce | flops 128 | bytes 1024 | tf_op jit(solution)/shard_map/psum | solution.py:30
  2182.1 53.6 %psum.143 = f32[128]{0:T(128)S(1)} all-reduce(f32[128]{0:T(128)S(1)} %psum.142), channel_id=1, replica_groups=mesh['clus'=16,'sub'=64] {'clus'}, use_global_device_ids=true, to_apply=%region_27.30 | all-reduce | flops 128 | bytes 1024 | tf_op jit(solution)/shard_map/psum | solution.py:34
  (134 shorter events, 39.5 us)
Async XLA Ops:
  6.5 283.9 %copy-start = (bf16[1,1024,1024]{2,1,0:T(8,128)(2,1)S(1)}, bf16[1,1024,1024]{2,1,0:T(8,128)(2,1)}, u32[]{:S(2)}) copy-start(bf16[1,1024,1024]{2,1,0:T(8,128)(2,1)} %param.11) | copy-start | bytes 6291460
  6.5 4.5 copy-start.24
  6.5 8.1 copy-start.12
  6.5 184.8 %copy-start.14 = (f32[96,96]{1,0:T(8,128)S(1)}, f32[96,96]{1,0:T(8,128)}, u32[]{:S(2)}) copy-start(f32[96,96]{1,0:T(8,128)} %param.17) | copy-start | bytes 110596
  6.5 280.8 %copy-start.11 = (f32[1,192,192]{2,1,0:T(8,128)S(1)}, f32[1,192,192]{2,1,0:T(8,128)}, u32[]{:S(2)}) copy-start(f32[1,192,192]{2,1,0:T(8,128)} %param.16) | copy-start | bytes 442372
  6.6 280.8 %all-reduce.6.cloned.1.call-start = ((), (), s32[]{:S(2)}) async-start(), calls=%async_computation.3 | async-start | bytes 196608 | tf_op jit(solution)/shard_map/psum | solution.py:30
  8.7 279.9 %copy-start.9 = (bf16[1,1024,128]{1,2,0:T(8,128)(2,1)}, bf16[1,1024,128]{1,2,0:T(8,128)(2,1)S(1)}, u32[]{:S(2)}) copy-start(bf16[1,1024,128]{1,2,0:T(8,128)(2,1)S(1)} %copy.26) | copy-start | bytes 786436
  8.7 279.9 %copy-start.1 = (bf16[1,192,896]{2,1,0:T(8,128)(2,1)S(1)}, bf16[1,192,896]{2,1,0:T(8,128)(2,1)}, u32[]{:S(2)}) copy-start(bf16[1,192,896]{2,1,0:T(8,128)(2,1)} %param.14) | copy-start | bytes 1032196
  8.8 181.7 %copy-start.19 = (f32[1024]{0:T(1024)}, f32[1024]{0:T(1024)S(1)}, u32[]{:S(2)}) copy-start(f32[1024]{0:T(1024)S(1)} %pad_maximum_fusion.5) | copy-start | bytes 12292
  11.0 3.6 copy-start.22
  299.4 54.2 %all-to-all-start = ((f32[64,32,128]{2,1,0:T(8,128)}), f32[64,32,128]{2,1,0:T(8,128)}, u32[]{:S(2)}, u32[]{:S(2)}) async-start(f32[64,32,128]{2,1,0:T(8,128)} %select_select_fusion.2), calls=%async_computation | async-start | bytes 2097152 | tf_op jit(solution)/shard_map/all_to_all | solution.py:64
  309.2 651.3 %all-reduce.8.cloned.1.call-start = ((), (), s32[]{:S(2)}) async-start(), calls=%async_computation.4 | async-start | bytes 196608 | tf_op jit(solution)/shard_map/psum | solution.py:30
  311.9 48.3 %collective-permute-start = (f32[64,128]{0,1:T(8,128)}, f32[64,128]{0,1:T(8,128)}, u32[]{:S(2)}, u32[]{:S(2)}) collective-permute-start(f32[64,128]{0,1:T(8,128)} %get-tuple-element.29), channel_id=1, source_target_pairs={{0,64},{64,128},{128,192},{192,256},{256,320},{320,384},{384,448},... | collective-permute-start | bytes 98312 | tf_op jit(solution)/shard_map/ppermute | solution.py:21
  325.9 34.2 %collective-permute-start.1 = (f32[64,128]{0,1:T(8,128)}, f32[64,128]{0,1:T(8,128)}, u32[]{:S(2)}, u32[]{:S(2)}) collective-permute-start(f32[64,128]{0,1:T(8,128)} %get-tuple-element.30), channel_id=1, source_target_pairs={{64,0},{128,64},{192,128},{256,192},{320,256},{384,320},{448,384},... | collective-permute-start | bytes 98312 | tf_op jit(solution)/shard_map/ppermute | solution.py:24
  538.3 3.1 copy-start.29
  540.4 0.9 copy-start.6
  542.5 422.0 %copy-start.7 = (f32[1024,128]{0,1:T(8,128)S(1)}, f32[1024,128]{0,1:T(8,128)}, u32[]{:S(2)}) copy-start(f32[1024,128]{0,1:T(8,128)} %copy-done.6) | copy-start | bytes 1572868
  963.7 0.8 copy-start.8
  1140.1 0.5 copy-start.31
  1141.3 0.6 copy-start.27
  1143.8 0.8 copy-start.3
  1144.6 5.6 copy-start.25
  1144.6 5.6 copy-start.26
  1152.7 63.1 %copy-start.21 = (pred[28]{0:T(512)(128)(4,1)S(1)}, pred[28]{0:T(512)(128)(4,1)}, u32[]{:S(2)}) copy-start(pred[28]{0:T(512)(128)(4,1)} %get-tuple-element.19) | copy-start | bytes 88
  1152.7 63.1 %copy-start.23 = (pred[28]{0:T(512)(128)(4,1)S(1)}, pred[28]{0:T(512)(128)(4,1)}, u32[]{:S(2)}) copy-start(pred[28]{0:T(512)(128)(4,1)} %copy-done.22) | copy-start | bytes 88
  1152.7 67.1 %copy-start.20 = (f32[1024]{0:T(1024)S(1)}, f32[1024]{0:T(1024)}, u32[]{:S(2)}) copy-start(f32[1024]{0:T(1024)} %copy-done.19) | copy-start | bytes 12292
  1152.7 60.4 %all-to-all-start.1 = ((f32[64,32,128]{2,1,0:T(8,128)}), f32[64,32,128]{2,1,0:T(8,128)}, u32[]{:S(2)}, u32[]{:S(2)}) async-start(f32[64,32,128]{2,1,0:T(8,128)} %select_select_fusion.1), calls=%async_computation.1 | async-start | bytes 2097152 | tf_op jit(solution)/shard_map/all_to_all | solution.py:64
  1161.7 648.8 %all-reduce.10.cloned.1.call-start = ((), (), s32[]{:S(2)}) async-start(), calls=%async_computation.5 | async-start | bytes 196608 | tf_op jit(solution)/shard_map/psum | solution.py:30
  1163.4 56.4 %collective-permute-start.2 = (f32[64,128]{0,1:T(8,128)}, f32[64,128]{0,1:T(8,128)S(1)}, u32[]{:S(2)}, u32[]{:S(2)}) collective-permute-start(f32[64,128]{0,1:T(8,128)} %get-tuple-element.27), channel_id=1, source_target_pairs={{0,64},{64,128},{128,192},{192,256},{256,320},{320,384},{384,448},... | collective-permute-start | bytes 98312 | tf_op jit(solution)/shard_map/ppermute | solution.py:21
  1165.3 223.0 %copy-start.32 = (f32[128]{0:T(128)S(1)}, f32[128]{0:T(128)}, u32[]{:S(2)}) copy-start(f32[128]{0:T(128)} %copy-done.31) | copy-start | bytes 1540
  1165.3 54.5 %collective-permute-start.3 = (f32[64,128]{0,1:T(8,128)}, f32[64,128]{0,1:T(8,128)}, u32[]{:S(2)}, u32[]{:S(2)}) collective-permute-start(f32[64,128]{0,1:T(8,128)} %get-tuple-element.28), channel_id=1, source_target_pairs={{64,0},{128,64},{192,128},{256,192},{320,256},{384,320},{448,384},... | collective-permute-start | bytes 98312 | tf_op jit(solution)/shard_map/ppermute | solution.py:24
  1219.8 170.9 %copy-start.13 = (bf16[1,6,896]{2,1,0:T(8,128)(2,1)S(1)}, bf16[1,6,896]{2,1,0:T(8,128)(2,1)}, u32[]{:S(2)}) copy-start(bf16[1,6,896]{2,1,0:T(8,128)(2,1)} %param.15) | copy-start | bytes 32260
  1219.8 168.5 %copy-start.18 = (f32[64,128]{0,1:T(8,128)}, f32[64,128]{0,1:T(8,128)S(1)}, u32[]{:S(2)}) copy-start(f32[64,128]{0,1:T(8,128)S(1)} %collective-permute-done.2) | copy-start | bytes 98308
  1388.3 161.1 %copy-start.15 = (f32[96,96]{1,0:T(8,128)S(1)}, f32[96,96]{1,0:T(8,128)}, u32[]{:S(2)}) copy-start(f32[96,96]{1,0:T(8,128)} %param.17) | copy-start | bytes 110596
  1390.7 0.8 copy-start.4
  1810.5 4.0 copy-start.5
  1813.7 0.8 copy-start.2
  1991.3 0.8 copy-start.10
  2000.2 60.3 %all-to-all-start.2 = ((f32[64,32,128]{2,1,0:T(8,128)}), f32[64,32,128]{2,1,0:T(8,128)}, u32[]{:S(2)}, u32[]{:S(2)}) async-start(f32[64,32,128]{2,1,0:T(8,128)} %select_select_fusion), calls=%async_computation.2 | async-start | bytes 2097152 | tf_op jit(solution)/shard_map/all_to_all | solution.py:64
  2011.4 55.7 %collective-permute-start.4 = (f32[64,128]{0,1:T(8,128)}, f32[64,128]{0,1:T(8,128)S(1)}, u32[]{:S(2)}, u32[]{:S(2)}) collective-permute-start(f32[64,128]{0,1:T(8,128)} %get-tuple-element.21), channel_id=1, source_target_pairs={{0,64},{64,128},{128,192},{192,256},{256,320},{320,384},{384,448},... | collective-permute-start | bytes 98312 | tf_op jit(solution)/shard_map/ppermute | solution.py:21
  2013.3 53.8 %collective-permute-start.5 = (f32[64,128]{0,1:T(8,128)}, f32[64,128]{0,1:T(8,128)S(1)}, u32[]{:S(2)}, u32[]{:S(2)}) collective-permute-start(f32[64,128]{0,1:T(8,128)} %get-tuple-element.22), channel_id=1, source_target_pairs={{64,0},{128,64},{192,128},{256,192},{320,256},{384,320},{448,384},... | collective-permute-start | bytes 98312 | tf_op jit(solution)/shard_map/ppermute | solution.py:24
  2063.2 172.5 %copy-start.16 = (f32[1,128,128]{1,2,0:T(8,128)S(1)}, f32[1,128,128]{1,2,0:T(8,128)}, u32[]{:S(2)}) copy-start(f32[1,128,128]{1,2,0:T(8,128)} %get-tuple-element.25) | copy-start | bytes 196612
  2063.2 172.5 %copy-start.17 = (f32[1,128,128]{1,2,0:T(8,128)S(1)}, f32[1,128,128]{1,2,0:T(8,128)}, u32[]{:S(2)}) copy-start(f32[1,128,128]{1,2,0:T(8,128)} %get-tuple-element.24) | copy-start | bytes 196612
  2063.2 172.5 %copy-start.28 = (f32[128]{0:T(128)S(1)}, f32[128]{0:T(128)}, u32[]{:S(2)}) copy-start(f32[128]{0:T(128)} %copy-done.27) | copy-start | bytes 1540
  2063.2 172.5 %copy-start.30 = (f32[128]{0:T(128)S(1)}, f32[128]{0:T(128)}, u32[]{:S(2)}) copy-start(f32[128]{0:T(128)} %copy-done.29) | copy-start | bytes 1540
Sparse Core Ops, SparseCore 0:
  11.1 276.1 all-reduce.5
  701.2 259.2 all-reduce.7
  1551.1 259.2 all-reduce.9
where the time goes:
time: 2250 us; the launch traced here: 2240 us
  blocking collectives  1350 us (60%)
  waiting for transfers between devices  726 us (32%)
  starting transfers between devices  52.4 us (2%)
  local copies, waits for them, and re-layouts  49.2 us (2%)
  other arithmetic  35 us (2%)
    psum x8, blocking collectives, cluster_sum(): return lax.psum(values, 'sub')  920 us
    psum x3, waiting for transfers between devices, cluster_sum(): return lax.psum(values, 'sub')  610 us
    psum x5, blocking collectives, global_sum(): return lax.psum(values, 'clus')  291 us
    all_gather x3, blocking collectives, global_gather(): return lax.all_gather(values, 'clus', axis=0, tiled=True)  135 us
    all_to_all x3, waiting for transfers between devices, swap_blocks(): lax.all_to_all(outgoing, 'sub', split_axis=0, concat_axis=0, tiled=True)  116 us
  transfers between devices with their start and end apart: 12, of which 6 were waited for; matrix products, arithmetic and copies ran while one was open for 2% of the time, Pallas kernels for 0%

commit v1 on v0

v1 whole, which is shorter than its diff:
```python
import jax
import jax.numpy as jnp
from jax import lax
from jax.experimental import pallas as pl
from jax.experimental.pallas import tpu as pltpu
from jax.sharding import PartitionSpec as P

FACE = 64
BLK = 32
MODES = 6
NIB = 28
RIM = 2 * FACE
CHUNK = 4
EXTRA = 16
GAMMA, DELTA, CROSS, CROSS_T = 6, 7, 8, 9

PRECISE = lax.Precision.HIGHEST
F32 = jnp.float32
BF16 = jnp.bfloat16


def split(value, parts):
    pieces = []
    for _ in range(parts):
        piece = value.astype(BF16)
        pieces.append(piece)
        value = value - piece.astype(F32)
    return pieces


def narrow_dot(narrow, value, parts, transposed=False):
    dims = (((0,), (0,)), ((), ())) if transposed else (((1,), (0,)), ((), ()))
    total = None
    for piece in reversed(split(value, parts)):
        term = lax.dot_general(narrow, piece, dims, preferred_element_type=F32)
        total = term if total is None else total + term
    return total


def wide_dot(first, second):
    return jnp.dot(first, second, precision=PRECISE, preferred_element_type=F32)


def column_sum(value):
    return jnp.sum(value, axis=0, keepdims=True)


def slot_row(index):
    return CHUNK * index + CHUNK - 1


def partner_rows(ids, incoming, block):
    target = ids[block]
    rows = incoming[jnp.maximum(target, 0)]
    return jnp.where(jnp.full(rows.shape, target, jnp.int32) >= 0, rows, 0.0)


def send_products(ids, products, out_blocks, low, high):
    low[...] = products[:FACE]
    high[...] = products[FACE:RIM]
    for block in range(NIB):
        target = ids[block]
        start = RIM + block * BLK

        @pl.when(target >= 0)
        def _():
            out_blocks[target] = products[start : start + BLK]


def set_row(ref, index, value):
    row = slot_row(index)
    ref[row : row + 1, :] = value


def one_hot(shape, test):
    rows = lax.broadcasted_iota(jnp.int32, shape, 0)
    columns = lax.broadcasted_iota(jnp.int32, shape, 1)
    return jnp.where(test(rows, columns), 1.0, 0.0)


def prepare_kernel(ids, rhs, cluster_basis, global_basis, inverse, global_inverse,
                   sums, basis, weight, solve, global_solve):
    cluster, last = ids[NIB], ids[NIB + 1]
    kc = cluster_basis.shape[0]
    rows = basis.shape[0]
    kg = global_inverse.shape[0]
    spread = one_hot((rows, kc), lambda i, j: i == j + j // (CHUNK - 1))
    spread_global = one_hot((rows, MODES), lambda i, j: i == CHUNK * j + CHUNK - 1)
    placed = jnp.dot(spread.astype(BF16), cluster_basis[...], preferred_element_type=F32)
    placed = placed + jnp.dot(
        spread_global.astype(BF16), global_basis[...], preferred_element_type=F32
    )
    basis[...] = placed.astype(BF16)
    shape = (FACE, weight.shape[1])
    weight[:FACE, :] = jnp.where(jnp.full(shape, cluster, jnp.int32) > 0, 0.5, 1.0)
    weight[FACE:RIM, :] = jnp.where(jnp.full(shape, cluster, jnp.int32) < last, 0.5, 1.0)
    for block in range(NIB):
        start = RIM + block * BLK
        weight[start : start + BLK, :] = jnp.where(
            jnp.full((BLK, weight.shape[1]), ids[block], jnp.int32) >= 0, 0.5, 1.0
        )
    weighted = weight[RIM:, :] * rhs[RIM:, :].astype(F32)
    sums[...] = narrow_dot(basis[...], weighted, 3)
    spread_t = one_hot((kc, rows), lambda i, j: j == i + i // (CHUNK - 1))
    solve[...] = wide_dot(wide_dot(spread, inverse[...]), spread_t)
    pick = one_hot(
        (rows, kg), lambda i, j: (i == CHUNK * (j - cluster * MODES) + CHUNK - 1)
        & (j >= cluster * MODES) & (j < (cluster + 1) * MODES)
    )
    place = one_hot(
        (kg, global_solve.shape[1]),
        lambda i, j: (j // EXTRA == i // MODES) & (j % EXTRA == i % MODES),
    )
    global_solve[...] = wide_dot(wide_dot(pick, global_inverse[...]), place)


def chunk_sum_kernel(parts, copies):
    rows, lanes = parts.shape
    tile = 2 * CHUNK
    total = jnp.sum(parts[...].reshape(rows // tile, tile, lanes), axis=0)
    total = total + pltpu.roll(total, CHUNK, 0)
    copies[...] = jnp.broadcast_to(total[None], (copies.shape[0] // tile, tile, lanes)).reshape(
        copies.shape
    )


def amounts(solve, global_solve, projection, global_projection):
    return wide_dot(solve[...], projection) + wide_dot(global_solve[...], global_projection)


def totals(gathered):
    rows, lanes = gathered.shape
    return jnp.sum(gathered[...].reshape(rows // EXTRA, EXTRA, lanes), axis=0)


def start_kernel(ids, rhs, operator, basis, weight, solve, global_solve, projection, gathered,
                 precond, products, sums, out_blocks, low, high):
    coarse = amounts(solve, global_solve, projection[...], gathered[...])
    extra = narrow_dot(basis[...], coarse, 3, transposed=True)
    precond[:RIM, :] = rhs[:RIM, :].astype(F32)
    precond[RIM:, :] = rhs[RIM:, :].astype(F32) + extra
    direction = precond[...]
    products[...] = narrow_dot(operator[...], direction, 1)
    send_products(ids, products, out_blocks, low, high)
    sums[...] = narrow_dot(basis[...], products[RIM:, :], 3)
    set_row(sums, GAMMA, column_sum(weight[...] * rhs[...].astype(F32) * direction))
    set_row(sums, DELTA, column_sum(direction * products[...]))


def store_applied(ids, applied, products, incoming, from_low, from_high):
    applied[:FACE, :] = products[:FACE, :] + from_low[...]
    applied[FACE:RIM, :] = products[FACE:RIM, :] + from_high[...]
    for block in range(NIB):
        start = RIM + block * BLK
        applied[start : start + BLK, :] = products[start : start + BLK, :] + partner_rows(
            ids, incoming, block
        )


def first_step_kernel(ids, rhs, operator, basis, weight, solve, global_solve,
                      projection, gathered, precond, products,
                      incoming, from_low, from_high, projection_a, gathered_a,
                      residual, applied, projection_new, gathered_new, scalars,
                      precond_new, products_new, sums, out_blocks, low, high):
    total = totals(gathered_a)
    gamma, curve = total[GAMMA : GAMMA + 1], total[DELTA : DELTA + 1]
    alpha = gamma / curve
    scalars[0:1, :] = gamma
    scalars[1:2, :] = curve
    scalars[2:3, :] = alpha
    projection_new[...] = projection[...] - alpha * projection_a[...]
    gathered_new[...] = gathered[...] - alpha * gathered_a[...]
    coarse = amounts(solve, global_solve, projection_new[...], gathered_new[...])
    extra = narrow_dot(basis[...], coarse, 3, transposed=True)
    store_applied(ids, applied, products, incoming, from_low, from_high)
    residual[...] = rhs[...].astype(F32) - alpha * applied[...]
    precond_new[:RIM, :] = residual[:RIM, :]
    precond_new[RIM:, :] = residual[RIM:, :] + extra
    products_new[...] = narrow_dot(operator[...], precond_new[...], 2)
    send_products(ids, products_new, out_blocks, low, high)
    sums[...] = narrow_dot(basis[...], products_new[RIM:, :], 3)
    set_row(sums, GAMMA, column_sum(weight[...] * residual[...] * precond_new[...]))
    set_row(sums, DELTA, column_sum(precond_new[...] * products_new[...]))
    set_row(sums, CROSS, column_sum(precond_new[...] * products[...]))
    set_row(sums, CROSS_T, column_sum(precond[...] * products_new[...]))


def conjugate(total, gamma_old, curve_old):
    gamma = total[GAMMA : GAMMA + 1]
    beta = gamma / gamma_old
    cross = total[CROSS : CROSS + 1] + total[CROSS_T : CROSS_T + 1]
    curve = total[DELTA : DELTA + 1] + beta * cross + beta * beta * curve_old
    return gamma, beta, curve, gamma / curve


def second_step_kernel(ids, operator, basis, weight, solve, global_solve,
                       residual, applied, projection, gathered, scalars,
                       precond_old, products_old, projection_old, gathered_old,
                       precond, products, incoming, from_low, from_high,
                       projection_a, gathered_a,
                       multipliers, direction, precond_new, scalars_new, copies, work, conj):
    gamma_old, curve_old = scalars[0:1, :], scalars[1:2, :]
    gamma, beta, curve, alpha = conjugate(totals(gathered_a), gamma_old, curve_old)
    scalars_new[0:1, :] = gamma
    scalars_new[1:2, :] = curve
    projection_new = projection[...] - alpha * (projection_a[...] + beta * projection_old[...])
    gathered_new = gathered[...] - alpha * (gathered_a[...] + beta * gathered_old[...])
    coarse = amounts(solve, global_solve, projection_new, gathered_new)
    extra = narrow_dot(basis[...], coarse, 3, transposed=True)
    direction[...] = precond[...] + beta * precond_old[...]
    multipliers[...] = scalars[2:3, :] * precond_old[...] + alpha * direction[...]
    conj[...] = products[...] + beta * products_old[...]
    store_applied(ids, work, products, incoming, from_low, from_high)
    work[...] = residual[...] - alpha * (work[...] + beta * applied[...])
    precond_new[:RIM, :] = work[:RIM, :]
    precond_new[RIM:, :] = work[RIM:, :] + extra
    gamma_part = column_sum(weight[...] * work[...] * precond_new[...])
    work[...] = narrow_dot(operator[...], precond_new[...], 2)
    rows = jnp.concatenate(
        [
            gamma_part,
            column_sum(precond_new[...] * work[...]),
            column_sum(precond_new[...] * conj[...]),
            column_sum(direction[...] * work[...]),
        ],
        axis=0,
    )
    tile = jnp.concatenate([rows, rows], axis=0)
    copies[...] = jnp.broadcast_to(
        tile[None], (copies.shape[0] // tile.shape[0],) + tile.shape
    ).reshape(copies.shape)


def last_step_kernel(multipliers, direction, precond, scalars, gathered, out):
    rows, lanes = gathered.shape
    tile = 2 * CHUNK
    total = jnp.sum(gathered[...].reshape(rows // tile, tile, lanes), axis=0)
    gamma = total[0:1]
    beta = gamma / scalars[0:1, :]
    curve = total[1:2] + beta * (total[2:3] + total[3:4]) + beta * beta * scalars[1:2, :]
    alpha = gamma / curve
    out[...] = multipliers[...] + alpha * (precond[...] + beta * direction[...])


def call(kernel, outs, args, scratch=(), smem=True):
    specs = [pl.BlockSpec(memory_space=pltpu.VMEM)] * len(args)
    if smem:
        specs[0] = pl.BlockSpec(memory_space=pltpu.SMEM)
    return pl.pallas_call(
        kernel,
        out_shape=[jax.ShapeDtypeStruct(shape, dtype) for shape, dtype in outs],
        in_specs=specs,
        out_specs=[pl.BlockSpec(memory_space=pltpu.VMEM)] * len(outs),
        scratch_shapes=[pltpu.VMEM(shape, dtype) for shape, dtype in scratch],
    )(*args)


def exchange(values):
    return lax.all_to_all(values, "sub", split_axis=0, concat_axis=0, tiled=True)


def on_device(
    dual_ops, dual_rhs, partner, cluster_basis, global_basis, cluster_inverse, global_inverse
):
    subs, clusters = lax.axis_size("sub"), lax.axis_size("clus")
    rhs = dual_rhs[0]
    operator = dual_ops[0]
    rows, lanes = rhs.shape
    partner_ids = partner[0]
    targets = jnp.where(partner_ids >= 0, partner_ids // NIB, -1).astype(jnp.int32)
    place = jnp.stack([lax.axis_index("clus"), jnp.int32(clusters - 1)]).astype(jnp.int32)
    ids = jnp.concatenate([targets, place, jnp.zeros((2,), jnp.int32)])
    n = subs * CHUNK
    vector = ((rows, lanes), F32)
    sums_out = ((n, lanes), F32)
    gathered_out = ((clusters * EXTRA, lanes), F32)
    scalar_out = ((8, lanes), F32)
    face = ((FACE, lanes), F32)
    blocks = ((subs, BLK, lanes), F32)

    def reduce_all(sums):
        (copies,) = call(chunk_sum_kernel, [sums_out], [exchange(sums)], smem=False)
        projection = exchange(copies)
        extra = lax.slice(
            projection, (CHUNK - 1, 0), (slot_row(EXTRA - 1) + 1, lanes), (CHUNK, 1)
        )
        return projection, lax.all_gather(extra, "clus", axis=0, tiled=True)

    def swap(out_blocks, low, high):
        up = [(i, i + 1) for i in range(clusters - 1)]
        down = [(i + 1, i) for i in range(clusters - 1)]
        from_low = lax.ppermute(high, "clus", up)
        from_high = lax.ppermute(low, "clus", down)
        return exchange(out_blocks), from_low, from_high

    sums, basis, weight, solve, global_solve = call(
        prepare_kernel,
        [sums_out, ((n, cluster_basis.shape[2]), BF16), vector, ((n, n), F32),
         ((n, clusters * EXTRA), F32)],
        [ids, rhs, cluster_basis[0], global_basis[0], cluster_inverse[0], global_inverse],
    )
    fixed = [basis, weight, solve, global_solve]
    projection, gathered = reduce_all(sums)

    precond, products, sums, out_blocks, low, high = call(
        start_kernel,
        [vector, vector, sums_out, blocks, face, face],
        [ids, rhs, operator, *fixed, projection, gathered],
    )
    swapped = swap(out_blocks, low, high)
    projection_a, gathered_a = reduce_all(sums)

    (residual, applied, projection_1, gathered_1, scalars, precond_1, products_1, sums,
     out_blocks, low, high) = call(
        first_step_kernel,
        [vector, vector, sums_out, gathered_out, scalar_out, vector, vector, sums_out,
         blocks, face, face],
        [ids, rhs, operator, *fixed, projection, gathered, precond, products, *swapped,
         projection_a, gathered_a],
    )
    swapped = swap(out_blocks, low, high)
    projection_b, gathered_b = reduce_all(sums)

    multipliers, direction, precond_2, scalars_1, copies = call(
        second_step_kernel,
        [vector, vector, vector, scalar_out, sums_out],
        [ids, operator, *fixed, residual, applied, projection_1, gathered_1, scalars,
         precond, products, projection_a, gathered_a, precond_1, products_1, *swapped,
         projection_b, gathered_b],
        scratch=[vector, vector],
    )
    (total,) = call(chunk_sum_kernel, [((2 * CHUNK, lanes), F32)], [exchange(copies)], smem=False)
    gathered_c = lax.all_gather(total, "clus", axis=0, tiled=True)
    (result,) = call(
        last_step_kernel, [vector], [multipliers, direction, precond_2, scalars_1, gathered_c],
        smem=False,
    )
    return result[None]


def solution(mesh):
    return jax.shard_map(
        on_device,
        mesh=mesh,
        in_specs=(
            P(("clus", "sub"), None, None),
            P(("clus", "sub"), None, None),
            P(("clus", "sub"), None),
            P(("clus", "sub"), None, None),
            P(("clus", "sub"), None, None),
            P("clus", None, None),
            P(),
        ),
        out_specs=P(("clus", "sub"), None, None),
        check_vma=False,
    )
```

time: 2250 us -> 364 us (0.16)
  blocking collectives: 1350 us -> 253 us
  waiting for transfers between devices: 726 us -> 46.1 us
  local copies, waits for them, and re-layouts: 49.2 us -> 2.01 us
  Pallas kernels: 0 us -> 35.3 us
  other arithmetic: 35 us -> 1.25 us
  starting transfers between devices: 52.4 us -> 25.2 us
    psum x13 -> x0, blocking collectives: 1210 us -> none  [the longest x8 920 us: cluster_sum(): return lax.psum(values, 'sub')]
    psum x3 -> x0, waiting for transfers between devices: 610 us -> none  [cluster_sum(): return lax.psum(values, 'sub')]
    all_to_all x0 -> x7, blocking collectives: none -> 171 us  [exchange(): lax.all_to_all(values, 'sub', split_axis=0, concat_axis=0, tiled=True)]
    all_to_all x3 -> x2, waiting for transfers between devices: 116 us -> 46 us  [exchange(): lax.all_to_all(values, 'sub', split_axis=0, concat_axis=0, tiled=True)]
    all_gather x3 -> x4, blocking collectives: 135 us -> 81.3 us  [the longest x3 60 us: reduce_all(): return (projection, lax.all_gather(extra, 'clus', axis=0, tiled=True))]
    pallas_call x0 -> x9, Pallas kernels: none -> 35.3 us  [call(): pl.pallas_call(kernel, out_shape=[jax.ShapeDtypeStruct(shape, dtype) for...]
  transfers between devices with their start and end apart: 12 -> 6, of which waited for: 6 -> 2; matrix products, arithmetic and copies ran while one was open for 2% -> 0% of each run, Pallas kernels for 0% -> 0%
where the time goes in v1:
time: 364 us; the launch traced here: 363 us
  blocking collectives  253 us (70%)
  waiting for transfers between devices  46.1 us (13%)
  Pallas kernels  35.3 us (10%)
  starting transfers between devices  25.2 us (7%)
    all_to_all x7, blocking collectives, exchange(): lax.all_to_all(values, 'sub', split_axis=0, concat_axis=0, tiled=True)  171 us
    all_gather x3, blocking collectives, reduce_all(): return (projection, lax.all_gather(extra, 'clus', axis=0, tiled=True))  60 us
    all_to_all x2, waiting for transfers between devices, exchange(): lax.all_to_all(values, 'sub', split_axis=0, concat_axis=0, tiled=True)  46 us
    pallas_call x9, Pallas kernels, call(): pl.pallas_call(kernel, out_shape=[jax.ShapeDtypeStruct(shape, dtype) for...  35.3 us
    all_gather x1, blocking collectives, on_device(): gathered_c = lax.all_gather(total, 'clus', axis=0, tiled=True)  21.3 us
    ppermute x2, starting transfers between devices, swap(): from_low = lax.ppermute(high, 'clus', up)  10.8 us
    all_to_all x2, starting transfers between devices, exchange(): lax.all_to_all(values, 'sub', split_axis=0, concat_axis=0, tiled=True)  10.6 us
  transfers between devices with their start and end apart: 6, of which 2 were waited for; matrix products, arithmetic and copies ran while one was open for 0% of the time, Pallas kernels for 0%

profile of v1, /device:TPU:1, one launch (start us, length us, event | category | flops | bytes accessed | tf_op | source)
XLA Modules:
  0.0 362.7 jit_solution(3999483879687454371)
XLA Ops:
  0.0 0.7 bitcast_select_fusion.1
  0.7 0.6 pad_add_fusion.ids
  1.3 4.0 %shard_map.73 = (f32[256,128]{1,0:T(8,128)}, bf16[256,896]{1,0:T(8,128)(2,1)}, f32[1024,128]{1,0:T(8,128)}, f32[256,256]{1,0:T(8,128)}, f32[256,256]{1,0:T(8,128)}) custom-call(s32[32]{0:T(128)} %pad_add_fusion.ids, bf16[1024,128]{1,0:T(8,128)(2,1)} %bitcast.34, bf16[192,896]{1,0:T(8,128)(2,1)} %bitcast.52, bf16[6,896]{1,0:T(8,128)(2,1)} %bitcast.58, ...), custom_call_target="tpu_custom_call" | custom-call | tf_op jit(solution)/shard_map/pallas_call | solution.py:249
  5.3 37.9 %all_to_all.87 = f32[64,4,128]{2,1,0:T(4,128)} all-to-all(f32[64,4,128]{2,1,0:T(4,128)} %bitcast.57), channel_id=1, replica_groups=mesh['clus'=16,'sub'=64] {'sub'}, dimensions={0} | all-to-all | bytes 262144 | tf_op jit(solution)/shard_map/all_to_all | solution.py:259
  43.2 1.6 shard_map.74
  44.8 21.3 %all_to_all.88 = f32[64,4,128]{2,1,0:T(4,128)S(1)} all-to-all(f32[64,4,128]{2,1,0:T(4,128)} %bitcast.46), channel_id=1, replica_groups=mesh['clus'=16,'sub'=64] {'sub'}, dimensions={0} | all-to-all | bytes 262144 | tf_op jit(solution)/shard_map/all_to_all | solution.py:259
  66.1 0.0 copy-start.3
  66.1 22.9 %all_gather.12.gathered = f32[256,128]{1,0:T(8,128)} all-gather(f32[16,128]{1,0:T(8,128)S(1)} %slice.9), channel_id=1, replica_groups=mesh['clus'=16,'sub'=64] {'clus'}, dimensions={0}, use_global_device_ids=true | all-gather | bytes 139264 | tf_op jit(solution)/shard_map/all_gather | solution.py:287
  89.0 0.0 copy-done.3
  89.0 6.6 %shard_map.75 = (f32[1024,128]{1,0:T(8,128)}, f32[1024,128]{1,0:T(8,128)}, f32[256,128]{1,0:T(8,128)}, f32[64,32,128]{2,1,0:T(8,128)}, f32[64,128]{1,0:T(8,128)}, /*index=5*/f32[64,128]{1,0:T(8,128)}) custom-call(s32[32]{0:T(128)} %pad_add_fusion.ids, bf16[1024,128]{1,0:T(8,128)(2,1)} %bitcast.35, bf16[1024,1024]{1,0:T(8,128)(2,1)} %bitcast.31, ...), custom_call_target="tpu_custom_call" | custom-call | tf_op jit(solution)/shard_map/pallas_call | solution.py:249
  95.5 0.0 copy-start.12
  95.5 0.0 copy-start.11
  95.5 22.4 %all_to_all.89 = f32[64,4,128]{2,1,0:T(4,128)} all-to-all(f32[64,4,128]{2,1,0:T(4,128)} %bitcast.56), channel_id=1, replica_groups=mesh['clus'=16,'sub'=64] {'sub'}, dimensions={0} | all-to-all | bytes 262144 | tf_op jit(solution)/shard_map/all_to_all | solution.py:259
  118.0 1.6 shard_map.76
  119.6 19.8 %all_to_all.90 = f32[64,4,128]{2,1,0:T(4,128)S(1)} all-to-all(f32[64,4,128]{2,1,0:T(4,128)} %bitcast.48), channel_id=1, replica_groups=mesh['clus'=16,'sub'=64] {'sub'}, dimensions={0} | all-to-all | bytes 262144 | tf_op jit(solution)/shard_map/all_to_all | solution.py:259
  139.4 0.0 copy-start.2
  139.4 6.0 %all-to-all-start.2 = ((f32[64,32,128]{2,1,0:T(8,128)}), f32[64,32,128]{2,1,0:T(8,128)S(1)}, u32[]{:S(2)}, u32[]{:S(2)}) async-start(f32[64,32,128]{2,1,0:T(8,128)} %get-tuple-element.39), calls=%async_computation.2 | async-start | bytes 2097152 | tf_op jit(solution)/shard_map/all_to_all | solution.py:259
  145.4 0.0 copy-done.12
  145.4 4.0 %collective-permute-start = (f32[64,128]{1,0:T(8,128)S(1)}, f32[64,128]{1,0:T(8,128)S(1)}, u32[]{:S(2)}, u32[]{:S(2)}) collective-permute-start(f32[64,128]{1,0:T(8,128)S(1)} %copy-done.12), channel_id=1, source_target_pairs={{0,64},{64,128},{128,192},{192,256},{256,320},{320,384},{384,448},... | collective-permute-start | bytes 98312 | tf_op jit(solution)/shard_map/ppermute | solution.py:292
  149.4 0.0 copy-done.11
  149.4 1.9 collective-permute-start.1
  151.3 18.7 %all_gather.13.gathered_a.gathered_old = f32[256,128]{1,0:T(8,128)} all-gather(f32[16,128]{1,0:T(8,128)S(1)} %slice.10), channel_id=1, replica_groups=mesh['clus'=16,'sub'=64] {'clus'}, dimensions={0}, use_global_device_ids=true | all-gather | bytes 139264 | tf_op jit(solution)/shard_map/all_gather | solution.py:287
  170.0 0.0 collective-permute-done.from_low
  170.0 0.0 copy-start.7
  170.0 0.0 collective-permute-done.1.from_high
  170.0 0.0 copy-start.8
  170.0 26.3 %all-to-all-done.2.incoming = f32[64,32,128]{2,1,0:T(8,128)S(1)} async-done(((f32[64,32,128]{2,1,0:T(8,128)}), f32[64,32,128]{2,1,0:T(8,128)S(1)}, u32[]{:S(2)}, u32[]{:S(2)}) %all-to-all-start.2) | async-done | bytes 1048608 | tf_op jit(solution)/shard_map/all_to_all | solution.py:259
  196.4 0.0 copy-start
  196.4 0.0 copy-done.2
  196.4 0.0 copy-done.7
  196.4 0.0 copy-done.8
  196.4 1.0 copy-done
  197.3 8.4 %shard_map.77 = (f32[1024,128]{1,0:T(8,128)}, f32[1024,128]{1,0:T(8,128)}, f32[256,128]{1,0:T(8,128)}, f32[256,128]{1,0:T(8,128)}, f32[8,128]{1,0:T(8,128)}, /*i...) custom-call(s32[32]{0:T(128)} %pad_add_fusion.ids, ...), custom_call_target="tpu_custom_call" | custom-call | tf_op jit(solution)/shard_map/pallas_call | solution.py:249
  205.7 0.0 copy-start.10
  205.7 0.0 copy-start.9
  205.7 23.4 %all_to_all.91 = f32[64,4,128]{2,1,0:T(4,128)} all-to-all(f32[64,4,128]{2,1,0:T(4,128)} %bitcast.55), channel_id=1, replica_groups=mesh['clus'=16,'sub'=64] {'sub'}, dimensions={0} | all-to-all | bytes 262144 | tf_op jit(solution)/shard_map/all_to_all | solution.py:259
  229.1 1.6 shard_map.78
  230.7 19.8 %all_to_all.92 = f32[64,4,128]{2,1,0:T(4,128)S(1)} all-to-all(f32[64,4,128]{2,1,0:T(4,128)} %bitcast.50), channel_id=1, replica_groups=mesh['clus'=16,'sub'=64] {'sub'}, dimensions={0} | all-to-all | bytes 262144 | tf_op jit(solution)/shard_map/all_to_all | solution.py:259
  250.6 0.0 copy-start.4
  250.6 4.7 %all-to-all-start.5 = ((f32[64,32,128]{2,1,0:T(8,128)}), f32[64,32,128]{2,1,0:T(8,128)S(1)}, u32[]{:S(2)}, u32[]{:S(2)}) async-start(f32[64,32,128]{2,1,0:T(8,128)} %get-tuple-element.50), calls=%async_computation.5 | async-start | bytes 2097152 | tf_op jit(solution)/shard_map/all_to_all | solution.py:259
  255.2 0.0 copy-done.10
  255.2 6.8 %collective-permute-start.2 = (f32[64,128]{1,0:T(8,128)S(1)}, f32[64,128]{1,0:T(8,128)S(1)}, u32[]{:S(2)}, u32[]{:S(2)}) collective-permute-start(f32[64,128]{1,0:T(8,128)S(1)} %copy-done.10), channel_id=1, source_target_pairs={{0,64},{64,128},{128,192},{192,256},{256,320},{320,384},{384,448},... | collective-permute-start | bytes 98312 | tf_op jit(solution)/shard_map/ppermute | solution.py:292
  262.0 0.0 copy-done.9
  262.0 1.9 collective-permute-start.3
  264.0 18.5 %all_gather.14.gathered_a = f32[256,128]{1,0:T(8,128)} all-gather(f32[16,128]{1,0:T(8,128)S(1)} %slice.11), channel_id=1, replica_groups=mesh['clus'=16,'sub'=64] {'clus'}, dimensions={0}, use_global_device_ids=true | all-gather | bytes 139264 | tf_op jit(solution)/shard_map/all_gather | solution.py:287
  282.5 0.0 collective-permute-done.2.from_low
  282.5 0.0 copy-start.5
  282.5 0.0 collective-permute-done.3.from_high
  282.5 0.0 copy-start.6
  282.5 19.7 %all-to-all-done.5.incoming = f32[64,32,128]{2,1,0:T(8,128)S(1)} async-done(((f32[64,32,128]{2,1,0:T(8,128)}), f32[64,32,128]{2,1,0:T(8,128)S(1)}, u32[]{:S(2)}, u32[]{:S(2)}) %all-to-all-start.5) | async-done | bytes 1048608 | tf_op jit(solution)/shard_map/all_to_all | solution.py:259
  302.2 0.0 copy-start.1
  302.2 0.0 copy-done.4
  302.2 0.0 copy-done.5
  302.2 0.0 copy-done.6
  302.2 1.0 copy-done.1
  303.2 7.7 %shard_map.79 = (f32[1024,128]{1,0:T(8,128)}, f32[1024,128]{1,0:T(8,128)}, f32[1024,128]{1,0:T(8,128)}, f32[8,128]{1,0:T(8,128)}, f32[256,128]{1,0:T(8,128)}) custom-call(s32[32]{0:T(128)} %pad_add_fusion.ids, bf16[1024,1024]{1,0:T(8,128)(2,1)} %bitcast.33, bf16[256,896]{1,0:T(8,128)(2,1)} %get-tuple-element.32.basis, f32[1024,128]{1,0:T(8,128)} %get-tuple-element.33.weight, ...), custom_call_target="tpu_custom_call" | custom-call | tf_op jit(solution)/shard_map/pallas_call | solution.py:249
  310.9 26.7 %all_to_all.93 = f32[64,4,128]{2,1,0:T(4,128)} all-to-all(f32[64,4,128]{2,1,0:T(4,128)} %bitcast.54), channel_id=1, replica_groups=mesh['clus'=16,'sub'=64] {'sub'}, dimensions={0} | all-to-all | bytes 262144 | tf_op jit(solution)/shard_map/all_to_all | solution.py:259
  337.6 1.5 shard_map.80
  339.1 21.3 %all_gather.15.gathered = f32[128,128]{1,0:T(8,128)} all-gather(f32[8,128]{1,0:T(8,128)} %shard_map.80), channel_id=1, replica_groups=mesh['clus'=16,'sub'=64] {'clus'}, dimensions={0}, use_global_device_ids=true | all-gather | bytes 69632 | tf_op jit(solution)/shard_map/all_gather | solution.py:333
  360.5 2.3 shard_map.81
  (4 shorter events, 0.0 us)
Async XLA Ops:
  66.1 22.9 %copy-start.3 = (f32[64,4,128]{2,1,0:T(4,128)}, f32[64,4,128]{2,1,0:T(4,128)S(1)}, u32[]{:S(2)}) copy-start(f32[64,4,128]{2,1,0:T(4,128)S(1)} %all_to_all.88) | copy-start | bytes 393220
  95.5 49.8 %copy-start.12 = (f32[64,128]{1,0:T(8,128)S(1)}, f32[64,128]{1,0:T(8,128)}, u32[]{:S(2)}) copy-start(f32[64,128]{1,0:T(8,128)} %get-tuple-element.40) | copy-start | bytes 98308
  95.5 53.8 %copy-start.11 = (f32[64,128]{1,0:T(8,128)S(1)}, f32[64,128]{1,0:T(8,128)}, u32[]{:S(2)}) copy-start(f32[64,128]{1,0:T(8,128)} %get-tuple-element.41) | copy-start | bytes 98308
  139.4 57.0 %copy-start.2 = (f32[64,4,128]{2,1,0:T(4,128)}, f32[64,4,128]{2,1,0:T(4,128)S(1)}, u32[]{:S(2)}) copy-start(f32[64,4,128]{2,1,0:T(4,128)S(1)} %all_to_all.90) | copy-start | bytes 393220
  139.4 56.9 %all-to-all-start.2 = ((f32[64,32,128]{2,1,0:T(8,128)}), f32[64,32,128]{2,1,0:T(8,128)S(1)}, u32[]{:S(2)}, u32[]{:S(2)}) async-start(f32[64,32,128]{2,1,0:T(8,128)} %get-tuple-element.39), calls=%async_computation.2 | async-start | bytes 2097152 | tf_op jit(solution)/shard_map/all_to_all | solution.py:259
  145.4 24.6 %collective-permute-start = (f32[64,128]{1,0:T(8,128)S(1)}, f32[64,128]{1,0:T(8,128)S(1)}, u32[]{:S(2)}, u32[]{:S(2)}) collective-permute-start(f32[64,128]{1,0:T(8,128)S(1)} %copy-done.12), channel_id=1, source_target_pairs={{0,64},{64,128},{128,192},{192,256},{256,320},{320,384},{384,448},... | collective-permute-start | bytes 98312 | tf_op jit(solution)/shard_map/ppermute | solution.py:292
  149.4 20.6 %collective-permute-start.1 = (f32[64,128]{1,0:T(8,128)S(1)}, f32[64,128]{1,0:T(8,128)S(1)}, u32[]{:S(2)}, u32[]{:S(2)}) collective-permute-start(f32[64,128]{1,0:T(8,128)S(1)} %copy-done.11), channel_id=1, source_target_pairs={{64,0},{128,64},{192,128},{256,192},{320,256},{384,320},{448,384},... | collective-permute-start | bytes 98312 | tf_op jit(solution)/shard_map/ppermute | solution.py:293
  170.0 26.3 %copy-start.7 = (f32[64,128]{1,0:T(8,128)}, f32[64,128]{1,0:T(8,128)S(1)}, u32[]{:S(2)}) copy-start(f32[64,128]{1,0:T(8,128)S(1)} %collective-permute-done.from_low) | copy-start | bytes 98308
  170.0 26.3 %copy-start.8 = (f32[64,128]{1,0:T(8,128)}, f32[64,128]{1,0:T(8,128)S(1)}, u32[]{:S(2)}) copy-start(f32[64,128]{1,0:T(8,128)S(1)} %collective-permute-done.1.from_high) | copy-start | bytes 98308
  196.4 1.0 copy-start
  205.7 49.5 %copy-start.10 = (f32[64,128]{1,0:T(8,128)S(1)}, f32[64,128]{1,0:T(8,128)}, u32[]{:S(2)}) copy-start(f32[64,128]{1,0:T(8,128)} %get-tuple-element.51) | copy-start | bytes 98308
  205.7 56.3 %copy-start.9 = (f32[64,128]{1,0:T(8,128)S(1)}, f32[64,128]{1,0:T(8,128)}, u32[]{:S(2)}) copy-start(f32[64,128]{1,0:T(8,128)} %get-tuple-element.52) | copy-start | bytes 98308
  250.6 51.6 %copy-start.4 = (f32[64,4,128]{2,1,0:T(4,128)}, f32[64,4,128]{2,1,0:T(4,128)S(1)}, u32[]{:S(2)}) copy-start(f32[64,4,128]{2,1,0:T(4,128)S(1)} %all_to_all.92) | copy-start | bytes 393220
  250.6 51.6 %all-to-all-start.5 = ((f32[64,32,128]{2,1,0:T(8,128)}), f32[64,32,128]{2,1,0:T(8,128)S(1)}, u32[]{:S(2)}, u32[]{:S(2)}) async-start(f32[64,32,128]{2,1,0:T(8,128)} %get-tuple-element.50), calls=%async_computation.5 | async-start | bytes 2097152 | tf_op jit(solution)/shard_map/all_to_all | solution.py:259
  255.2 27.2 %collective-permute-start.2 = (f32[64,128]{1,0:T(8,128)S(1)}, f32[64,128]{1,0:T(8,128)S(1)}, u32[]{:S(2)}, u32[]{:S(2)}) collective-permute-start(f32[64,128]{1,0:T(8,128)S(1)} %copy-done.10), channel_id=1, source_target_pairs={{0,64},{64,128},{128,192},{192,256},{256,320},{320,384},{384,448},... | collective-permute-start | bytes 98312 | tf_op jit(solution)/shard_map/ppermute | solution.py:292
  262.0 20.4 %collective-permute-start.3 = (f32[64,128]{1,0:T(8,128)S(1)}, f32[64,128]{1,0:T(8,128)S(1)}, u32[]{:S(2)}, u32[]{:S(2)}) collective-permute-start(f32[64,128]{1,0:T(8,128)S(1)} %copy-done.9), channel_id=1, source_target_pairs={{64,0},{128,64},{192,128},{256,192},{320,256},{384,320},{448,384},... | collective-permute-start | bytes 98312 | tf_op jit(solution)/shard_map/ppermute | solution.py:293
  282.5 19.8 %copy-start.5 = (f32[64,128]{1,0:T(8,128)}, f32[64,128]{1,0:T(8,128)S(1)}, u32[]{:S(2)}) copy-start(f32[64,128]{1,0:T(8,128)S(1)} %collective-permute-done.2.from_low) | copy-start | bytes 98308
  282.5 19.7 %copy-start.6 = (f32[64,128]{1,0:T(8,128)}, f32[64,128]{1,0:T(8,128)S(1)}, u32[]{:S(2)}) copy-start(f32[64,128]{1,0:T(8,128)S(1)} %collective-permute-done.3.from_high) | copy-start | bytes 98308
  302.2 1.0 copy-start.1

commit v2 on v1

--- a/solution.py
+++ b/solution.py
@@ -10,6 +10,7 @@
 MODES = 6
 NIB = 28
 RIM = 2 * FACE
+NEAR = 4
 CHUNK = 4
 EXTRA = 16
 GAMMA, DELTA, CROSS, CROSS_T = 6, 7, 8, 9
@@ -28,12 +29,13 @@
     return pieces
 
 
-def narrow_dot(narrow, value, parts, transposed=False):
-    dims = (((0,), (0,)), ((), ())) if transposed else (((1,), (0,)), ((), ()))
-    total = None
-    for piece in reversed(split(value, parts)):
-        term = lax.dot_general(narrow, piece, dims, preferred_element_type=F32)
-        total = term if total is None else total + term
+def narrow_dot(narrow, value, parts):
+    lanes = value.shape[1]
+    pieces = jnp.concatenate(split(value, parts), axis=1)
+    product = jnp.dot(narrow, pieces, preferred_element_type=F32)
+    total = product[:, (parts - 1) * lanes :]
+    for part in reversed(range(parts - 1)):
+        total = total + product[:, part * lanes : (part + 1) * lanes]
     return total
 
 
@@ -79,7 +81,7 @@
 
 
 def prepare_kernel(ids, rhs, cluster_basis, global_basis, inverse, global_inverse,
-                   sums, basis, weight, solve, global_solve):
+                   sums, basis, basis_t, weight, solve, global_solve):
     cluster, last = ids[NIB], ids[NIB + 1]
     kc = cluster_basis.shape[0]
     rows = basis.shape[0]
@@ -91,6 +93,7 @@
         spread_global.astype(BF16), global_basis[...], preferred_element_type=F32
     )
     basis[...] = placed.astype(BF16)
+    basis_t[...] = placed.T.astype(BF16)
     shape = (FACE, weight.shape[1])
     weight[:FACE, :] = jnp.where(jnp.full(shape, cluster, jnp.int32) > 0, 0.5, 1.0)
     weight[FACE:RIM, :] = jnp.where(jnp.full(shape, cluster, jnp.int32) < last, 0.5, 1.0)
@@ -119,9 +122,12 @@
     tile = 2 * CHUNK
     total = jnp.sum(parts[...].reshape(rows // tile, tile, lanes), axis=0)
     total = total + pltpu.roll(total, CHUNK, 0)
-    copies[...] = jnp.broadcast_to(total[None], (copies.shape[0] // tile, tile, lanes)).reshape(
-        copies.shape
-    )
+    if copies.shape[0] <= tile:
+        copies[...] = total[: copies.shape[0]]
+    else:
+        copies[...] = jnp.broadcast_to(
+            total[None], (copies.shape[0] // tile, tile, lanes)
+        ).reshape(copies.shape)
 
 
 def amounts(solve, global_solve, projection, global_projection):
@@ -133,10 +139,10 @@
     return jnp.sum(gathered[...].reshape(rows // EXTRA, EXTRA, lanes), axis=0)
 
 
-def start_kernel(ids, rhs, operator, basis, weight, solve, global_solve, projection, gathered,
+def start_kernel(ids, rhs, operator, basis, basis_t, weight, solve, global_solve, projection, gathered,
                  precond, products, sums, out_blocks, low, high):
     coarse = amounts(solve, global_solve, projection[...], gathered[...])
-    extra = narrow_dot(basis[...], coarse, 3, transposed=True)
+    extra = narrow_dot(basis_t[...], coarse, 3)
     precond[:RIM, :] = rhs[:RIM, :].astype(F32)
     precond[RIM:, :] = rhs[RIM:, :].astype(F32) + extra
     direction = precond[...]
@@ -157,7 +163,7 @@
         )
 
 
-def first_step_kernel(ids, rhs, operator, basis, weight, solve, global_solve,
+def first_step_kernel(ids, rhs, operator, basis, basis_t, weight, solve, global_solve,
                       projection, gathered, precond, products,
                       incoming, from_low, from_high, projection_a, gathered_a,
                       residual, applied, projection_new, gathered_new, scalars,
@@ -171,7 +177,7 @@
     projection_new[...] = projection[...] - alpha * projection_a[...]
     gathered_new[...] = gathered[...] - alpha * gathered_a[...]
     coarse = amounts(solve, global_solve, projection_new[...], gathered_new[...])
-    extra = narrow_dot(basis[...], coarse, 3, transposed=True)
+    extra = narrow_dot(basis_t[...], coarse, 3)
     store_applied(ids, applied, products, incoming, from_low, from_high)
     residual[...] = rhs[...].astype(F32) - alpha * applied[...]
     precond_new[:RIM, :] = residual[:RIM, :]
@@ -193,7 +199,7 @@
     return gamma, beta, curve, gamma / curve
 
 
-def second_step_kernel(ids, operator, basis, weight, solve, global_solve,
+def second_step_kernel(ids, operator, basis, basis_t, weight, solve, global_solve,
                        residual, applied, projection, gathered, scalars,
                        precond_old, products_old, projection_old, gathered_old,
                        precond, products, incoming, from_low, from_high,
@@ -206,7 +212,7 @@
     projection_new = projection[...] - alpha * (projection_a[...] + beta * projection_old[...])
     gathered_new = gathered[...] - alpha * (gathered_a[...] + beta * gathered_old[...])
     coarse = amounts(solve, global_solve, projection_new, gathered_new)
-    extra = narrow_dot(basis[...], coarse, 3, transposed=True)
+    extra = narrow_dot(basis_t[...], coarse, 3)
     direction[...] = precond[...] + beta * precond_old[...]
     multipliers[...] = scalars[2:3, :] * precond_old[...] + alpha * direction[...]
     conj[...] = products[...] + beta * products_old[...]
@@ -253,6 +259,15 @@
         out_specs=[pl.BlockSpec(memory_space=pltpu.VMEM)] * len(outs),
         scratch_shapes=[pltpu.VMEM(shape, dtype) for shape, dtype in scratch],
     )(*args)
+
+
+def gather_subs(values):
+    subs = lax.axis_size("sub")
+    rows_of = [[far * NEAR + near for near in range(NEAR)] for far in range(subs // NEAR)]
+    columns_of = [[far * NEAR + near for far in range(subs // NEAR)] for near in range(NEAR)]
+    for groups in (rows_of, columns_of):
+        values = lax.all_gather(values, "sub", axis=0, tiled=True, axis_index_groups=groups)
+    return values
 
 
 def exchange(values):
@@ -278,9 +293,10 @@
     face = ((FACE, lanes), F32)
     blocks = ((subs, BLK, lanes), F32)
 
-    def reduce_all(sums):
-        (copies,) = call(chunk_sum_kernel, [sums_out], [exchange(sums)], smem=False)
-        projection = exchange(copies)
+    def reduce_all(sums, beside):
+        shape = sums_out if not beside else ((CHUNK, lanes), F32)
+        (copies,) = call(chunk_sum_kernel, [shape], [exchange(sums)], smem=False)
+        projection = gather_subs(copies) if beside else exchange(copies)
         extra = lax.slice(
             projection, (CHUNK - 1, 0), (slot_row(EXTRA - 1) + 1, lanes), (CHUNK, 1)
         )
@@ -293,14 +309,14 @@
         from_high = lax.ppermute(low, "clus", down)
         return exchange(out_blocks), from_low, from_high
 
-    sums, basis, weight, solve, global_solve = call(
+    sums, basis, basis_t, weight, solve, global_solve = call(
         prepare_kernel,
-        [sums_out, ((n, cluster_basis.shape[2]), BF16), vector, ((n, n), F32),
+        [sums_out, ((n, cluster_basis.shape[2]), BF16), ((cluster_basis.shape[2], n), BF16), vector, ((n, n), F32),
          ((n, clusters * EXTRA), F32)],
         [ids, rhs, cluster_basis[0], global_basis[0], cluster_inverse[0], global_inverse],
     )
-    fixed = [basis, weight, solve, global_solve]
-    projection, gathered = reduce_all(sums)
+    fixed = [basis, basis_t, weight, solve, global_solve]
+    projection, gathered = reduce_all(sums, False)
 
     precond, products, sums, out_blocks, low, high = call(
         start_kernel,
@@ -308,7 +324,7 @@
         [ids, rhs, operator, *fixed, projection, gathered],
     )
     swapped = swap(out_blocks, low, high)
-    projection_a, gathered_a = reduce_all(sums)
+    projection_a, gathered_a = reduce_all(sums, True)
 
     (residual, applied, projection_1, gathered_1, scalars, precond_1, products_1, sums,
      out_blocks, low, high) = call(
@@ -319,7 +335,7 @@
          projection_a, gathered_a],
     )
     swapped = swap(out_blocks, low, high)
-    projection_b, gathered_b = reduce_all(sums)
+    projection_b, gathered_b = reduce_all(sums, True)
 
     multipliers, direction, precond_2, scalars_1, copies = call(
         second_step_kernel,

time: 364 us -> 404 us (1.11)
  blocking collectives: 253 us -> 344 us
  waiting for transfers between devices: 46.1 us -> 0.02 us
    all_gather x0 -> x4, blocking collectives: none -> 113 us  [gather_subs(): lax.all_gather(values, 'sub', axis=0, tiled=True, axis_index_groups=groups)]
    all_to_all x2, waiting for transfers between devices: 46 us -> 0.01 us  [exchange(): lax.all_to_all(values, 'sub', split_axis=0, concat_axis=0, tiled=True)]
    all_to_all x7 -> x5, blocking collectives: 171 us -> 140 us  [exchange(): lax.all_to_all(values, 'sub', split_axis=0, concat_axis=0, tiled=True)]
    all_gather x3, blocking collectives: 60 us -> 72.5 us  [reduce_all(): return (projection, lax.all_gather(extra, 'clus', axis=0, tiled=True))]
  transfers between devices with their start and end apart: 6 -> 6, of which waited for: 2 -> 0; matrix products, arithmetic and copies ran while one was open for 0% -> 0% of each run, Pallas kernels for 0% -> 1%
where the time goes in v2:
time: 404 us; the launch traced here: 403 us
  blocking collectives  344 us (85%)
  Pallas kernels  33.3 us (8%)
  starting transfers between devices  22.2 us (5%)
    all_to_all x5, blocking collectives, exchange(): lax.all_to_all(values, 'sub', split_axis=0, concat_axis=0, tiled=True)  140 us
    all_gather x4, blocking collectives, gather_subs(): lax.all_gather(values, 'sub', axis=0, tiled=True, axis_index_groups=groups)  113 us
    all_gather x3, blocking collectives, reduce_all(): return (projection, lax.all_gather(extra, 'clus', axis=0, tiled=True))  72.5 us
    pallas_call x9, Pallas kernels, call(): pl.pallas_call(kernel, out_shape=[jax.ShapeDtypeStruct(shape, dtype) for...  33.3 us
    all_gather x1, blocking collectives, on_device(): gathered_c = lax.all_gather(total, 'clus', axis=0, tiled=True)  19.6 us
    all_to_all x2, starting transfers between devices, exchange(): lax.all_to_all(values, 'sub', split_axis=0, concat_axis=0, tiled=True)  10.5 us
  transfers between devices with their start and end apart: 6, of which 0 were waited for; matrix products, arithmetic and copies ran while one was open for 0% of the time, Pallas kernels for 1%

profile of v2, /device:TPU:1, one launch (start us, length us, event | category | flops | bytes accessed | tf_op | source)
XLA Modules:
  0.0 403.5 jit_solution(6396474564383120109)
XLA Ops:
  0.0 0.7 bitcast_select_fusion.1
  0.7 0.6 pad_add_fusion.ids
  1.3 4.0 shard_map.73
  5.2 37.9 %all_to_all.65 = f32[64,4,128]{2,1,0:T(4,128)} all-to-all(f32[64,4,128]{2,1,0:T(4,128)} %bitcast.49), channel_id=1, replica_groups=mesh['clus'=16,'sub'=64] {'sub'}, dimensions={0} | all-to-all | bytes 262144 | tf_op jit(solution)/shard_map/all_to_all | solution.py:274
  43.2 1.6 shard_map.74
  44.7 21.3 %all_to_all.66 = f32[64,4,128]{2,1,0:T(4,128)S(1)} all-to-all(f32[64,4,128]{2,1,0:T(4,128)} %bitcast.43), channel_id=1, replica_groups=mesh['clus'=16,'sub'=64] {'sub'}, dimensions={0} | all-to-all | bytes 262144 | tf_op jit(solution)/shard_map/all_to_all | solution.py:274
  66.0 0.0 copy-start.3
  66.0 22.9 %all_gather.24.gathered = f32[256,128]{1,0:T(8,128)} all-gather(f32[16,128]{1,0:T(8,128)S(1)} %slice.9), channel_id=1, replica_groups=mesh['clus'=16,'sub'=64] {'clus'}, dimensions={0}, use_global_device_ids=true | all-gather | bytes 139264 | tf_op jit(solution)/shard_map/all_gather | solution.py:303
  88.9 0.0 copy-done.3
  88.9 6.4 %shard_map.75 = (f32[1024,128]{1,0:T(8,128)}, f32[1024,128]{1,0:T(8,128)}, f32[256,128]{1,0:T(8,128)}, f32[64,32,128]{2,1,0:T(8,128)}, f32[64,128]{1,0:T(8,128)}, /*index=5*/f32[64,128]{1,0:T(8,128)}) custom-call(s32[32]{0:T(128)} %pad_add_fusion.ids, bf16[1024,128]{1,0:T(8,128)(2,1)} %bitcast.35, bf16[1024,1024]{1,0:T(8,128)(2,1)} %bitcast.31, ...), custom_call_target="tpu_custom_call" | custom-call | tf_op jit(solution)/shard_map/pallas_call | solution.py:255
  95.3 0.0 copy-start.12
  95.3 0.0 copy-start.11
  95.3 22.4 %all_to_all.67 = f32[64,4,128]{2,1,0:T(4,128)} all-to-all(f32[64,4,128]{2,1,0:T(4,128)} %bitcast.50), channel_id=1, replica_groups=mesh['clus'=16,'sub'=64] {'sub'}, dimensions={0} | all-to-all | bytes 262144 | tf_op jit(solution)/shard_map/all_to_all | solution.py:274
  117.7 4.7 %all-to-all-start.2 = ((f32[64,32,128]{2,1,0:T(8,128)}), f32[64,32,128]{2,1,0:T(8,128)S(1)}, u32[]{:S(2)}, u32[]{:S(2)}) async-start(f32[64,32,128]{2,1,0:T(8,128)} %get-tuple-element.41), calls=%async_computation.2 | async-start | bytes 2097152 | tf_op jit(solution)/shard_map/all_to_all | solution.py:274
  122.4 0.0 copy-done.12
  122.4 3.4 collective-permute-start
  125.8 0.0 copy-done.11
  125.8 1.9 collective-permute-start.1
  127.7 1.5 shard_map.76
  129.3 9.4 %all-gather = f32[4,4,128]{2,1,0:T(4,128)S(1)} all-gather(f32[1,4,128]{2,1,0:T(4,128)} %bitcast.54), channel_id=1, replica_groups={{0,1,2,3},{4,5,6,7},{8,9,10,11},{12,13,14,15},{16,17,18,19},{20,21,22,2..., dimensions={0}, use_global_device_ids=true | all-gather | bytes 10240 | tf_op jit(solution)/shard_map/all_gather | solution.py:269
  138.7 47.4 %all_gather.26.projection_a.projection_old = f32[256,128]{1,0:T(8,128)S(1)} all-gather(f32[16,128]{1,0:T(8,128)S(1)} %bitcast.51), channel_id=1, replica_groups={{0,4,8,12,16,20,24,28,32,36,40,44,48,52,56,60},{1,5,9,13,17,21,25,29,33..., dimensions={0}, use_global_device_ids=true | all-gather | bytes 139264 | tf_op jit(solution)/shard_map/all_gather | solution.py:269
  186.1 0.0 copy-start.2
  186.1 24.6 %all_gather.27.gathered_a.gathered_old = f32[256,128]{1,0:T(8,128)} all-gather(f32[16,128]{1,0:T(8,128)S(1)} %slice.10), channel_id=1, replica_groups=mesh['clus'=16,'sub'=64] {'clus'}, dimensions={0}, use_global_device_ids=true | all-gather | bytes 139264 | tf_op jit(solution)/shard_map/all_gather | solution.py:303
  210.7 0.0 collective-permute-done.from_low
  210.8 0.0 copy-start.7
  210.8 0.0 collective-permute-done.1.from_high
  210.8 0.0 copy-start.8
  210.8 0.0 all-to-all-done.2.incoming
  210.8 0.0 copy-start.1
  210.8 0.0 copy-done.2
  210.8 0.6 copy-done.7
  211.4 0.0 copy-done.8
  211.4 0.4 copy-done.1
  211.8 7.5 %shard_map.77 = (f32[1024,128]{1,0:T(8,128)}, f32[1024,128]{1,0:T(8,128)}, f32[256,128]{1,0:T(8,128)}, f32[256,128]{1,0:T(8,128)}, f32[8,128]{1,0:T(8,128)}, /*i...) custom-call(s32[32]{0:T(128)} %pad_add_fusion.ids, ...), custom_call_target="tpu_custom_call" | custom-call | tf_op jit(solution)/shard_map/pallas_call | solution.py:255
  219.3 0.0 copy-start.10
  219.3 0.0 copy-start.9
  219.3 29.1 %all_to_all.68 = f32[64,4,128]{2,1,0:T(4,128)} all-to-all(f32[64,4,128]{2,1,0:T(4,128)} %bitcast.48), channel_id=1, replica_groups=mesh['clus'=16,'sub'=64] {'sub'}, dimensions={0} | all-to-all | bytes 262144 | tf_op jit(solution)/shard_map/all_to_all | solution.py:274
  248.4 5.8 %all-to-all-start.4 = ((f32[64,32,128]{2,1,0:T(8,128)}), f32[64,32,128]{2,1,0:T(8,128)S(1)}, u32[]{:S(2)}, u32[]{:S(2)}) async-start(f32[64,32,128]{2,1,0:T(8,128)} %get-tuple-element.52), calls=%async_computation.4 | async-start | bytes 2097152 | tf_op jit(solution)/shard_map/all_to_all | solution.py:274
  254.2 0.0 copy-done.10
  254.2 4.6 %collective-permute-start.2 = (f32[64,128]{1,0:T(8,128)S(1)}, f32[64,128]{1,0:T(8,128)S(1)}, u32[]{:S(2)}, u32[]{:S(2)}) collective-permute-start(f32[64,128]{1,0:T(8,128)S(1)} %copy-done.10), channel_id=1, source_target_pairs={{0,64},{64,128},{128,192},{192,256},{256,320},{320,384},{384,448},... | collective-permute-start | bytes 98312 | tf_op jit(solution)/shard_map/ppermute | solution.py:308
  258.8 0.0 copy-done.9
  258.8 1.9 collective-permute-start.3
  260.7 1.5 shard_map.78
  262.3 9.3 %all-gather.1 = f32[4,4,128]{2,1,0:T(4,128)S(1)} all-gather(f32[1,4,128]{2,1,0:T(4,128)} %bitcast.55), channel_id=1, replica_groups={{0,1,2,3},{4,5,6,7},{8,9,10,11},{12,13,14,15},{16,17,18,19},{20,21,22,2..., dimensions={0}, use_global_device_ids=true | all-gather | bytes 10240 | tf_op jit(solution)/shard_map/all_gather | solution.py:269
  271.6 46.3 %all_gather.29.projection_a = f32[256,128]{1,0:T(8,128)S(1)} all-gather(f32[16,128]{1,0:T(8,128)S(1)} %bitcast.52), channel_id=1, replica_groups={{0,4,8,12,16,20,24,28,32,36,40,44,48,52,56,60},{1,5,9,13,17,21,25,29,33..., dimensions={0}, use_global_device_ids=true | all-gather | bytes 139264 | tf_op jit(solution)/shard_map/all_gather | solution.py:269
  317.9 0.0 copy-start.4
  318.0 25.0 %all_gather.30.gathered_a = f32[256,128]{1,0:T(8,128)} all-gather(f32[16,128]{1,0:T(8,128)S(1)} %slice.11), channel_id=1, replica_groups=mesh['clus'=16,'sub'=64] {'clus'}, dimensions={0}, use_global_device_ids=true | all-gather | bytes 139264 | tf_op jit(solution)/shard_map/all_gather | solution.py:303
  343.0 0.0 collective-permute-done.2.from_low
  343.0 0.0 copy-start.5
  343.0 0.0 collective-permute-done.3.from_high
  343.0 0.0 copy-start.6
  343.0 0.0 all-to-all-done.4.incoming
  343.0 0.0 copy-start
  343.0 0.0 copy-done.4
  343.0 0.6 copy-done.5
  343.6 0.0 copy-done.6
  343.6 0.4 copy-done
  344.0 7.0 %shard_map.79 = (f32[1024,128]{1,0:T(8,128)}, f32[1024,128]{1,0:T(8,128)}, f32[1024,128]{1,0:T(8,128)}, f32[8,128]{1,0:T(8,128)}, f32[256,128]{1,0:T(8,128)}) custom-call(s32[32]{0:T(128)} %pad_add_fusion.ids, bf16[1024,1024]{1,0:T(8,128)(2,1)} %bitcast.33, bf16[256,896]{1,0:T(8,128)(2,1)} %get-tuple-element.33.basis, ...), custom_call_target="tpu_custom_call" | custom-call | tf_op jit(solution)/shard_map/pallas_call | solution.py:255
  351.0 29.1 %all_to_all.69 = f32[64,4,128]{2,1,0:T(4,128)} all-to-all(f32[64,4,128]{2,1,0:T(4,128)} %bitcast.47), channel_id=1, replica_groups=mesh['clus'=16,'sub'=64] {'sub'}, dimensions={0} | all-to-all | bytes 262144 | tf_op jit(solution)/shard_map/all_to_all | solution.py:274
  380.1 1.5 shard_map.80
  381.7 19.6 %all_gather.31.gathered = f32[128,128]{1,0:T(8,128)} all-gather(f32[8,128]{1,0:T(8,128)} %shard_map.80), channel_id=1, replica_groups=mesh['clus'=16,'sub'=64] {'clus'}, dimensions={0}, use_global_device_ids=true | all-gather | bytes 69632 | tf_op jit(solution)/shard_map/all_gather | solution.py:349
  401.2 2.3 shard_map.81
  (4 shorter events, 0.0 us)
Async XLA Ops:
  66.0 22.9 %copy-start.3 = (f32[64,4,128]{2,1,0:T(4,128)}, f32[64,4,128]{2,1,0:T(4,128)S(1)}, u32[]{:S(2)}) copy-start(f32[64,4,128]{2,1,0:T(4,128)S(1)} %all_to_all.66) | copy-start | bytes 393220
  95.3 27.1 %copy-start.12 = (f32[64,128]{1,0:T(8,128)S(1)}, f32[64,128]{1,0:T(8,128)}, u32[]{:S(2)}) copy-start(f32[64,128]{1,0:T(8,128)} %get-tuple-element.42) | copy-start | bytes 98308
  95.3 30.5 %copy-start.11 = (f32[64,128]{1,0:T(8,128)S(1)}, f32[64,128]{1,0:T(8,128)}, u32[]{:S(2)}) copy-start(f32[64,128]{1,0:T(8,128)} %get-tuple-element.43) | copy-start | bytes 98308
  117.7 93.0 %all-to-all-start.2 = ((f32[64,32,128]{2,1,0:T(8,128)}), f32[64,32,128]{2,1,0:T(8,128)S(1)}, u32[]{:S(2)}, u32[]{:S(2)}) async-start(f32[64,32,128]{2,1,0:T(8,128)} %get-tuple-element.41), calls=%async_computation.2 | async-start | bytes 2097152 | tf_op jit(solution)/shard_map/all_to_all | solution.py:274
  122.4 88.4 %collective-permute-start = (f32[64,128]{1,0:T(8,128)S(1)}, f32[64,128]{1,0:T(8,128)S(1)}, u32[]{:S(2)}, u32[]{:S(2)}) collective-permute-start(f32[64,128]{1,0:T(8,128)S(1)} %copy-done.12), channel_id=1, source_target_pairs={{0,64},{64,128},{128,192},{192,256},{256,320},{320,384},{384,448},... | collective-permute-start | bytes 98312 | tf_op jit(solution)/shard_map/ppermute | solution.py:308
  125.8 85.0 %collective-permute-start.1 = (f32[64,128]{1,0:T(8,128)S(1)}, f32[64,128]{1,0:T(8,128)S(1)}, u32[]{:S(2)}, u32[]{:S(2)}) collective-permute-start(f32[64,128]{1,0:T(8,128)S(1)} %copy-done.11), channel_id=1, source_target_pairs={{64,0},{128,64},{192,128},{256,192},{320,256},{384,320},{448,384},... | collective-permute-start | bytes 98312 | tf_op jit(solution)/shard_map/ppermute | solution.py:309
  186.1 24.7 %copy-start.2 = (f32[256,128]{1,0:T(8,128)}, f32[256,128]{1,0:T(8,128)S(1)}, u32[]{:S(2)}) copy-start(f32[256,128]{1,0:T(8,128)S(1)} %all_gather.26.projection_a.projection_old) | copy-start | bytes 393220
  210.8 0.6 copy-start.7
  210.8 0.6 copy-start.8
  210.8 1.0 copy-start.1
  219.3 35.0 %copy-start.10 = (f32[64,128]{1,0:T(8,128)S(1)}, f32[64,128]{1,0:T(8,128)}, u32[]{:S(2)}) copy-start(f32[64,128]{1,0:T(8,128)} %get-tuple-element.53) | copy-start | bytes 98308
  219.3 39.5 %copy-start.9 = (f32[64,128]{1,0:T(8,128)S(1)}, f32[64,128]{1,0:T(8,128)}, u32[]{:S(2)}) copy-start(f32[64,128]{1,0:T(8,128)} %get-tuple-element.54) | copy-start | bytes 98308
  248.4 94.6 %all-to-all-start.4 = ((f32[64,32,128]{2,1,0:T(8,128)}), f32[64,32,128]{2,1,0:T(8,128)S(1)}, u32[]{:S(2)}, u32[]{:S(2)}) async-start(f32[64,32,128]{2,1,0:T(8,128)} %get-tuple-element.52), calls=%async_computation.4 | async-start | bytes 2097152 | tf_op jit(solution)/shard_map/all_to_all | solution.py:274
  254.2 88.7 %collective-permute-start.2 = (f32[64,128]{1,0:T(8,128)S(1)}, f32[64,128]{1,0:T(8,128)S(1)}, u32[]{:S(2)}, u32[]{:S(2)}) collective-permute-start(f32[64,128]{1,0:T(8,128)S(1)} %copy-done.10), channel_id=1, source_target_pairs={{0,64},{64,128},{128,192},{192,256},{256,320},{320,384},{384,448},... | collective-permute-start | bytes 98312 | tf_op jit(solution)/shard_map/ppermute | solution.py:308
  258.8 84.2 %collective-permute-start.3 = (f32[64,128]{1,0:T(8,128)S(1)}, f32[64,128]{1,0:T(8,128)S(1)}, u32[]{:S(2)}, u32[]{:S(2)}) collective-permute-start(f32[64,128]{1,0:T(8,128)S(1)} %copy-done.9), channel_id=1, source_target_pairs={{64,0},{128,64},{192,128},{256,192},{320,256},{384,320},{448,384},... | collective-permute-start | bytes 98312 | tf_op jit(solution)/shard_map/ppermute | solution.py:309
  317.9 25.1 %copy-start.4 = (f32[256,128]{1,0:T(8,128)}, f32[256,128]{1,0:T(8,128)S(1)}, u32[]{:S(2)}) copy-start(f32[256,128]{1,0:T(8,128)S(1)} %all_gather.29.projection_a) | copy-start | bytes 393220
  343.0 0.6 copy-start.5
  343.0 0.6 copy-start.6
  343.0 1.0 copy-start

commit v3 on v2

--- a/solution.py
+++ b/solution.py
@@ -128,6 +128,21 @@
         copies[...] = jnp.broadcast_to(
             total[None], (copies.shape[0] // tile, tile, lanes)
         ).reshape(copies.shape)
+
+
+def far_sum_kernel(parts, copies):
+    rows, lanes = parts.shape
+    far = lax.axis_size("sub") // NEAR
+    total = jnp.sum(parts[...].reshape(far, rows // far, lanes), axis=0)
+    copies[...] = jnp.broadcast_to(total[None], (far,) + total.shape).reshape(rows, lanes)
+
+
+def near_sum_kernel(parts, total, extra):
+    rows, lanes = total.shape
+    total[...] = jnp.sum(parts[...].reshape(NEAR, rows, lanes), axis=0)
+    for index in range(EXTRA):
+        row = slot_row(index)
+        extra[index : index + 1, :] = total[row : row + 1, :]
 
 
 def amounts(solve, global_solve, projection, global_projection):
@@ -261,13 +276,20 @@
     )(*args)
 
 
-def gather_subs(values):
+def near_groups():
     subs = lax.axis_size("sub")
-    rows_of = [[far * NEAR + near for near in range(NEAR)] for far in range(subs // NEAR)]
-    columns_of = [[far * NEAR + near for far in range(subs // NEAR)] for near in range(NEAR)]
-    for groups in (rows_of, columns_of):
-        values = lax.all_gather(values, "sub", axis=0, tiled=True, axis_index_groups=groups)
-    return values
+    return [[far * NEAR + near for near in range(NEAR)] for far in range(subs // NEAR)]
+
+
+def far_groups():
+    subs = lax.axis_size("sub")
+    return [[far * NEAR + near for far in range(subs // NEAR)] for near in range(NEAR)]
+
+
+def exchange_far(values):
+    return lax.all_to_all(
+        values, "sub", split_axis=0, concat_axis=0, tiled=True, axis_index_groups=far_groups()
+    )
 
 
 def exchange(values):
@@ -293,12 +315,22 @@
     face = ((FACE, lanes), F32)
     blocks = ((subs, BLK, lanes), F32)
 
-    def reduce_all(sums, beside):
-        shape = sums_out if not beside else ((CHUNK, lanes), F32)
-        (copies,) = call(chunk_sum_kernel, [shape], [exchange(sums)], smem=False)
-        projection = gather_subs(copies) if beside else exchange(copies)
+    def reduce_first(sums):
+        (copies,) = call(chunk_sum_kernel, [sums_out], [exchange(sums)], smem=False)
+        projection = exchange(copies)
         extra = lax.slice(
             projection, (CHUNK - 1, 0), (slot_row(EXTRA - 1) + 1, lanes), (CHUNK, 1)
+        )
+        return projection, lax.all_gather(extra, "clus", axis=0, tiled=True)
+
+    def reduce_beside(sums):
+        (copies,) = call(far_sum_kernel, [sums_out], [exchange_far(sums)], smem=False)
+        column = exchange_far(copies)
+        parts = lax.all_gather(
+            column, "sub", axis=0, tiled=True, axis_index_groups=near_groups()
+        )
+        projection, extra = call(
+            near_sum_kernel, [sums_out, ((EXTRA, lanes), F32)], [parts], smem=False
         )
         return projection, lax.all_gather(extra, "clus", axis=0, tiled=True)
 
@@ -316,7 +348,7 @@
         [ids, rhs, cluster_basis[0], global_basis[0], cluster_inverse[0], global_inverse],
     )
     fixed = [basis, basis_t, weight, solve, global_solve]
-    projection, gathered = reduce_all(sums, False)
+    projection, gathered = reduce_first(sums)
 
     precond, products, sums, out_blocks, low, high = call(
         start_kernel,
@@ -324,7 +356,7 @@
         [ids, rhs, operator, *fixed, projection, gathered],
     )
     swapped = swap(out_blocks, low, high)
-    projection_a, gathered_a = reduce_all(sums, True)
+    projection_a, gathered_a = reduce_beside(sums)
 
     (residual, applied, projection_1, gathered_1, scalars, precond_1, products_1, sums,
      out_blocks, low, high) = call(
@@ -335,7 +367,7 @@
          projection_a, gathered_a],
     )
     swapped = swap(out_blocks, low, high)
-    projection_b, gathered_b = reduce_all(sums, True)
+    projection_b, gathered_b = reduce_beside(sums)
 
     multipliers, direction, precond_2, scalars_1, copies = call(
         second_step_kernel,

time: 404 us -> 350 us (0.87)
  blocking collectives: 344 us -> 266 us
  waiting for transfers between devices: 0.02 us -> 14.2 us
  starting transfers between devices: 22.2 us -> 28.7 us
    all_gather x7 -> x5, blocking collectives: 185 us -> 88.8 us  [the longest x2 38.9 us: reduce_beside(): return (projection, lax.all_gather(extra, 'clus', axis=0, tiled=True))]
    all_to_all x0 -> x4, blocking collectives: none -> 69.3 us  [exchange_far(): lax.all_to_all(values, 'sub', split_axis=0, concat_axis=0, tiled=True, ax...]
    all_to_all x5 -> x3, blocking collectives: 140 us -> 86.7 us  [exchange(): lax.all_to_all(values, 'sub', split_axis=0, concat_axis=0, tiled=True)]
    all_to_all x2, waiting for transfers between devices: 0.01 us -> 14.2 us  [exchange(): lax.all_to_all(values, 'sub', split_axis=0, concat_axis=0, tiled=True)]
    all_to_all x2, starting transfers between devices: 10.5 us -> 14.6 us  [exchange(): lax.all_to_all(values, 'sub', split_axis=0, concat_axis=0, tiled=True)]
    pallas_call x9 -> x11, Pallas kernels: 33.3 us -> 36.9 us  [call(): pl.pallas_call(kernel, out_shape=[jax.ShapeDtypeStruct(shape, dtype) for...]
  transfers between devices with their start and end apart: 6 -> 6, of which waited for: 0 -> 2; matrix products, arithmetic and copies ran while one was open for 0% -> 0% of each run, Pallas kernels for 1% -> 1%
where the time goes in v3:
time: 350 us; the launch traced here: 349 us
  blocking collectives  266 us (76%)
  Pallas kernels  36.9 us (11%)
  starting transfers between devices  28.7 us (8%)
  waiting for transfers between devices  14.2 us (4%)
    all_to_all x3, blocking collectives, exchange(): lax.all_to_all(values, 'sub', split_axis=0, concat_axis=0, tiled=True)  86.7 us
    all_to_all x4, blocking collectives, exchange_far(): lax.all_to_all(values, 'sub', split_axis=0, concat_axis=0, tiled=True, ax...  69.3 us
    all_gather x2, blocking collectives, reduce_beside(): return (projection, lax.all_gather(extra, 'clus', axis=0, tiled=True))  38.9 us
    pallas_call x11, Pallas kernels, call(): pl.pallas_call(kernel, out_shape=[jax.ShapeDtypeStruct(shape, dtype) for...  36.9 us
    all_gather x2, blocking collectives, reduce_beside(): lax.all_gather(column, 'sub', axis=0, tiled=True, axis_index_groups=near_...  27 us
    all_gather x1, blocking collectives, reduce_first(): return (projection, lax.all_gather(extra, 'clus', axis=0, tiled=True))  22.9 us
    all_gather x1, blocking collectives, on_device(): gathered_c = lax.all_gather(total, 'clus', axis=0, tiled=True)  21.1 us
    all_to_all x2, starting transfers between devices, exchange(): lax.all_to_all(values, 'sub', split_axis=0, concat_axis=0, tiled=True)  14.6 us
  transfers between devices with their start and end apart: 6, of which 2 were waited for; matrix products, arithmetic and copies ran while one was open for 0% of the time, Pallas kernels for 1%

profile of v3, /device:TPU:1, one launch (start us, length us, event | category | flops | bytes accessed | tf_op | source)
XLA Modules:
  0.0 349.0 jit_solution(16463514239295828889)
XLA Ops:
  0.0 0.7 bitcast_select_fusion.1
  0.7 0.6 pad_add_fusion.ids
  1.3 4.0 %shard_map.73 = (f32[256,128]{1,0:T(8,128)}, bf16[256,896]{1,0:T(8,128)(2,1)}, bf16[896,256]{1,0:T(8,128)(2,1)}, f32[1024,128]{1,0:T(8,128)}, f32[256,256]{1,0:T(8,128)}, /*index=5*/f32[256,256]{1,0:T(8,128)}) custom-call(s32[32]{0:T(128)} %pad_add_fusion.ids, bf16[1024,128]{1,0:T(8,128)(2,1)} %bitcast.34, bf16[192,896]{1,0:T(8,128)(2,1)} %bitcast.49, ...), custom_call_target="tpu_custom_call" | custom-call | tf_op jit(solution)/shard_map/pallas_call | solution.py:270
  5.2 37.9 %all_to_all.89 = f32[64,4,128]{2,1,0:T(4,128)} all-to-all(f32[64,4,128]{2,1,0:T(4,128)} %bitcast.53), channel_id=1, replica_groups=mesh['clus'=16,'sub'=64] {'sub'}, dimensions={0} | all-to-all | bytes 262144 | tf_op jit(solution)/shard_map/all_to_all | solution.py:296
  43.2 1.6 shard_map.74
  44.7 21.3 %all_to_all.90 = f32[64,4,128]{2,1,0:T(4,128)S(1)} all-to-all(f32[64,4,128]{2,1,0:T(4,128)} %bitcast.43), channel_id=1, replica_groups=mesh['clus'=16,'sub'=64] {'sub'}, dimensions={0} | all-to-all | bytes 262144 | tf_op jit(solution)/shard_map/all_to_all | solution.py:296
  66.0 0.0 copy-start.2
  66.0 22.9 %all_gather.18.gathered = f32[256,128]{1,0:T(8,128)} all-gather(f32[16,128]{1,0:T(8,128)S(1)} %slice.3), channel_id=1, replica_groups=mesh['clus'=16,'sub'=64] {'clus'}, dimensions={0}, use_global_device_ids=true | all-gather | bytes 139264 | tf_op jit(solution)/shard_map/all_gather | solution.py:324
  88.9 0.0 copy-done.2
  88.9 6.4 %shard_map.75 = (f32[1024,128]{1,0:T(8,128)}, f32[1024,128]{1,0:T(8,128)}, f32[256,128]{1,0:T(8,128)}, f32[64,32,128]{2,1,0:T(8,128)}, f32[64,128]{1,0:T(8,128)}, /*index=5*/f32[64,128]{1,0:T(8,128)}) custom-call(s32[32]{0:T(128)} %pad_add_fusion.ids, bf16[1024,128]{1,0:T(8,128)(2,1)} %bitcast.35, bf16[1024,1024]{1,0:T(8,128)(2,1)} %bitcast.31, ...), custom_call_target="tpu_custom_call" | custom-call | tf_op jit(solution)/shard_map/pallas_call | solution.py:270
  95.3 0.0 copy-start.10
  95.3 0.0 copy-start.9
  95.3 16.9 %all_to_all.91 = f32[16,16,128]{2,1,0:T(8,128)} all-to-all(f32[16,16,128]{2,1,0:T(8,128)} %bitcast.54), channel_id=1, replica_groups={{0,4,8,12,16,20,24,28,32,36,40,44,48,52,56,60},{1,5,9,13,17,21,25,29,33..., dimensions={0} | all-to-all | bytes 262144 | tf_op jit(solution)/shard_map/all_to_all | solution.py:290
  112.2 1.6 shard_map.76
  113.8 18.0 %all_to_all.92 = f32[16,16,128]{2,1,0:T(8,128)S(1)} all-to-all(f32[16,16,128]{2,1,0:T(8,128)} %bitcast.45), channel_id=1, replica_groups={{0,4,8,12,16,20,24,28,32,36,40,44,48,52,56,60},{1,5,9,13,17,21,25,29,33..., dimensions={0} | all-to-all | bytes 262144 | tf_op jit(solution)/shard_map/all_to_all | solution.py:290
  131.8 7.8 %all-to-all-start.2 = ((f32[64,32,128]{2,1,0:T(8,128)}), f32[64,32,128]{2,1,0:T(8,128)S(1)}, u32[]{:S(2)}, u32[]{:S(2)}) async-start(f32[64,32,128]{2,1,0:T(8,128)} %get-tuple-element.45), calls=%async_computation.2 | async-start | bytes 2097152 | tf_op jit(solution)/shard_map/all_to_all | solution.py:296
  139.6 0.0 copy-done.10
  139.6 3.0 collective-permute-start
  142.6 0.0 copy-done.9
  142.6 1.9 collective-permute-start.1
  144.5 13.2 %all_gather.19.parts = f32[1024,128]{1,0:T(8,128)} all-gather(f32[256,128]{1,0:T(8,128)S(1)} %bitcast.40), channel_id=1, replica_groups={{0,1,2,3},{4,5,6,7},{8,9,10,11},{12,13,14,15},{16,17,18,19},{20,21,22,2..., dimensions={0}, use_global_device_ids=true | all-gather | bytes 655360 | tf_op jit(solution)/shard_map/all_gather | solution.py:329
  157.7 1.7 shard_map.77
  159.5 19.9 %all_gather.20.gathered_a.gathered_old = f32[256,128]{1,0:T(8,128)} all-gather(f32[16,128]{1,0:T(8,128)} %get-tuple-element.50), channel_id=1, replica_groups=mesh['clus'=16,'sub'=64] {'clus'}, dimensions={0}, use_global_device_ids=true | all-gather | bytes 139264 | tf_op jit(solution)/shard_map/all_gather | solution.py:335
  179.4 0.0 collective-permute-done.from_low
  179.4 0.0 copy-start.5
  179.4 0.0 collective-permute-done.1.from_high
  179.4 0.0 copy-start.6
  179.4 11.4 %all-to-all-done.2.incoming = f32[64,32,128]{2,1,0:T(8,128)S(1)} async-done(((f32[64,32,128]{2,1,0:T(8,128)}), f32[64,32,128]{2,1,0:T(8,128)S(1)}, u32[]{:S(2)}, u32[]{:S(2)}) %all-to-all-start.2) | async-done | bytes 1048608 | tf_op jit(solution)/shard_map/all_to_all | solution.py:296
  190.8 0.0 copy-start.1
  190.8 0.0 copy-done.5
  190.8 0.0 copy-done.6
  190.8 1.0 copy-done.1
  191.7 7.5 %shard_map.78 = (f32[1024,128]{1,0:T(8,128)}, f32[1024,128]{1,0:T(8,128)}, f32[256,128]{1,0:T(8,128)}, f32[256,128]{1,0:T(8,128)}, f32[8,128]{1,0:T(8,128)}, /*i...) custom-call(s32[32]{0:T(128)} %pad_add_fusion.ids, ...), custom_call_target="tpu_custom_call" | custom-call | tf_op jit(solution)/shard_map/pallas_call | solution.py:270
  199.3 0.0 copy-start.8
  199.3 0.0 copy-start.7
  199.3 18.5 %all_to_all.93 = f32[16,16,128]{2,1,0:T(8,128)} all-to-all(f32[16,16,128]{2,1,0:T(8,128)} %bitcast.52), channel_id=1, replica_groups={{0,4,8,12,16,20,24,28,32,36,40,44,48,52,56,60},{1,5,9,13,17,21,25,29,33..., dimensions={0} | all-to-all | bytes 262144 | tf_op jit(solution)/shard_map/all_to_all | solution.py:290
  217.8 1.6 shard_map.79
  219.4 15.9 %all_to_all.94 = f32[16,16,128]{2,1,0:T(8,128)S(1)} all-to-all(f32[16,16,128]{2,1,0:T(8,128)} %bitcast.47), channel_id=1, replica_groups={{0,4,8,12,16,20,24,28,32,36,40,44,48,52,56,60},{1,5,9,13,17,21,25,29,33..., dimensions={0} | all-to-all | bytes 262144 | tf_op jit(solution)/shard_map/all_to_all | solution.py:290
  235.3 6.8 %all-to-all-start.5 = ((f32[64,32,128]{2,1,0:T(8,128)}), f32[64,32,128]{2,1,0:T(8,128)S(1)}, u32[]{:S(2)}, u32[]{:S(2)}) async-start(f32[64,32,128]{2,1,0:T(8,128)} %get-tuple-element.58), calls=%async_computation.5 | async-start | bytes 2097152 | tf_op jit(solution)/shard_map/all_to_all | solution.py:296
  242.1 0.0 copy-done.8
  242.1 7.3 %collective-permute-start.2 = (f32[64,128]{1,0:T(8,128)S(1)}, f32[64,128]{1,0:T(8,128)S(1)}, u32[]{:S(2)}, u32[]{:S(2)}) collective-permute-start(f32[64,128]{1,0:T(8,128)S(1)} %copy-done.8), channel_id=1, source_target_pairs={{0,64},{64,128},{128,192},{192,256},{256,320},{320,384},{384,448},... | collective-permute-start | bytes 98312 | tf_op jit(solution)/shard_map/ppermute | solution.py:340
  249.4 0.0 copy-done.7
  249.4 1.9 collective-permute-start.3
  251.3 13.8 %all_gather.21.parts = f32[1024,128]{1,0:T(8,128)} all-gather(f32[256,128]{1,0:T(8,128)S(1)} %bitcast.41), channel_id=1, replica_groups={{0,1,2,3},{4,5,6,7},{8,9,10,11},{12,13,14,15},{16,17,18,19},{20,21,22,2..., dimensions={0}, use_global_device_ids=true | all-gather | bytes 655360 | tf_op jit(solution)/shard_map/all_gather | solution.py:329
  265.1 1.7 shard_map.80
  266.8 19.0 %all_gather.22.gathered_a = f32[256,128]{1,0:T(8,128)} all-gather(f32[16,128]{1,0:T(8,128)} %get-tuple-element.63), channel_id=1, replica_groups=mesh['clus'=16,'sub'=64] {'clus'}, dimensions={0}, use_global_device_ids=true | all-gather | bytes 139264 | tf_op jit(solution)/shard_map/all_gather | solution.py:335
  285.8 0.0 collective-permute-done.2.from_low
  285.8 0.0 copy-start.3
  285.8 0.0 collective-permute-done.3.from_high
  285.8 0.0 copy-start.4
  285.8 2.8 all-to-all-done.5.incoming
  288.6 0.0 copy-start
  288.6 0.0 copy-done.3
  288.6 0.0 copy-done.4
  288.6 1.0 copy-done
  289.6 7.0 %shard_map.81 = (f32[1024,128]{1,0:T(8,128)}, f32[1024,128]{1,0:T(8,128)}, f32[1024,128]{1,0:T(8,128)}, f32[8,128]{1,0:T(8,128)}, f32[256,128]{1,0:T(8,128)}) custom-call(s32[32]{0:T(128)} %pad_add_fusion.ids, bf16[1024,1024]{1,0:T(8,128)(2,1)} %bitcast.33, bf16[256,896]{1,0:T(8,128)(2,1)} %get-tuple-element.37.basis, ...), custom_call_target="tpu_custom_call" | custom-call | tf_op jit(solution)/shard_map/pallas_call | solution.py:270
  296.6 27.5 %all_to_all.95 = f32[64,4,128]{2,1,0:T(4,128)} all-to-all(f32[64,4,128]{2,1,0:T(4,128)} %bitcast.51), channel_id=1, replica_groups=mesh['clus'=16,'sub'=64] {'sub'}, dimensions={0} | all-to-all | bytes 262144 | tf_op jit(solution)/shard_map/all_to_all | solution.py:296
  324.2 1.5 shard_map.82
  325.7 21.1 %all_gather.23.gathered = f32[128,128]{1,0:T(8,128)} all-gather(f32[8,128]{1,0:T(8,128)} %shard_map.82), channel_id=1, replica_groups=mesh['clus'=16,'sub'=64] {'clus'}, dimensions={0}, use_global_device_ids=true | all-gather | bytes 69632 | tf_op jit(solution)/shard_map/all_gather | solution.py:381
  346.8 2.3 shard_map.83
  (2 shorter events, 0.0 us)
Async XLA Ops:
  66.0 22.9 %copy-start.2 = (f32[64,4,128]{2,1,0:T(4,128)}, f32[64,4,128]{2,1,0:T(4,128)S(1)}, u32[]{:S(2)}) copy-start(f32[64,4,128]{2,1,0:T(4,128)S(1)} %all_to_all.90) | copy-start | bytes 393220
  95.3 44.3 %copy-start.10 = (f32[64,128]{1,0:T(8,128)S(1)}, f32[64,128]{1,0:T(8,128)}, u32[]{:S(2)}) copy-start(f32[64,128]{1,0:T(8,128)} %get-tuple-element.46) | copy-start | bytes 98308
  95.3 47.3 %copy-start.9 = (f32[64,128]{1,0:T(8,128)S(1)}, f32[64,128]{1,0:T(8,128)}, u32[]{:S(2)}) copy-start(f32[64,128]{1,0:T(8,128)} %get-tuple-element.47) | copy-start | bytes 98308
  131.8 59.0 %all-to-all-start.2 = ((f32[64,32,128]{2,1,0:T(8,128)}), f32[64,32,128]{2,1,0:T(8,128)S(1)}, u32[]{:S(2)}, u32[]{:S(2)}) async-start(f32[64,32,128]{2,1,0:T(8,128)} %get-tuple-element.45), calls=%async_computation.2 | async-start | bytes 2097152 | tf_op jit(solution)/shard_map/all_to_all | solution.py:296
  139.6 39.8 %collective-permute-start = (f32[64,128]{1,0:T(8,128)S(1)}, f32[64,128]{1,0:T(8,128)S(1)}, u32[]{:S(2)}, u32[]{:S(2)}) collective-permute-start(f32[64,128]{1,0:T(8,128)S(1)} %copy-done.10), channel_id=1, source_target_pairs={{0,64},{64,128},{128,192},{192,256},{256,320},{320,384},{384,448},... | collective-permute-start | bytes 98312 | tf_op jit(solution)/shard_map/ppermute | solution.py:340
  142.6 36.8 %collective-permute-start.1 = (f32[64,128]{1,0:T(8,128)S(1)}, f32[64,128]{1,0:T(8,128)S(1)}, u32[]{:S(2)}, u32[]{:S(2)}) collective-permute-start(f32[64,128]{1,0:T(8,128)S(1)} %copy-done.9), channel_id=1, source_target_pairs={{64,0},{128,64},{192,128},{256,192},{320,256},{384,320},{448,384},... | collective-permute-start | bytes 98312 | tf_op jit(solution)/shard_map/ppermute | solution.py:341
  179.4 11.4 %copy-start.5 = (f32[64,128]{1,0:T(8,128)}, f32[64,128]{1,0:T(8,128)S(1)}, u32[]{:S(2)}) copy-start(f32[64,128]{1,0:T(8,128)S(1)} %collective-permute-done.from_low) | copy-start | bytes 98308
  179.4 11.4 %copy-start.6 = (f32[64,128]{1,0:T(8,128)}, f32[64,128]{1,0:T(8,128)S(1)}, u32[]{:S(2)}) copy-start(f32[64,128]{1,0:T(8,128)S(1)} %collective-permute-done.1.from_high) | copy-start | bytes 98308
  190.8 1.0 copy-start.1
  199.3 42.8 %copy-start.8 = (f32[64,128]{1,0:T(8,128)S(1)}, f32[64,128]{1,0:T(8,128)}, u32[]{:S(2)}) copy-start(f32[64,128]{1,0:T(8,128)} %get-tuple-element.59) | copy-start | bytes 98308
  199.3 50.1 %copy-start.7 = (f32[64,128]{1,0:T(8,128)S(1)}, f32[64,128]{1,0:T(8,128)}, u32[]{:S(2)}) copy-start(f32[64,128]{1,0:T(8,128)} %get-tuple-element.60) | copy-start | bytes 98308
  235.3 53.3 %all-to-all-start.5 = ((f32[64,32,128]{2,1,0:T(8,128)}), f32[64,32,128]{2,1,0:T(8,128)S(1)}, u32[]{:S(2)}, u32[]{:S(2)}) async-start(f32[64,32,128]{2,1,0:T(8,128)} %get-tuple-element.58), calls=%async_computation.5 | async-start | bytes 2097152 | tf_op jit(solution)/shard_map/all_to_all | solution.py:296
  242.1 43.7 %collective-permute-start.2 = (f32[64,128]{1,0:T(8,128)S(1)}, f32[64,128]{1,0:T(8,128)S(1)}, u32[]{:S(2)}, u32[]{:S(2)}) collective-permute-start(f32[64,128]{1,0:T(8,128)S(1)} %copy-done.8), channel_id=1, source_target_pairs={{0,64},{64,128},{128,192},{192,256},{256,320},{320,384},{384,448},... | collective-permute-start | bytes 98312 | tf_op jit(solution)/shard_map/ppermute | solution.py:340
  249.4 36.4 %collective-permute-start.3 = (f32[64,128]{1,0:T(8,128)S(1)}, f32[64,128]{1,0:T(8,128)S(1)}, u32[]{:S(2)}, u32[]{:S(2)}) collective-permute-start(f32[64,128]{1,0:T(8,128)S(1)} %copy-done.7), channel_id=1, source_target_pairs={{64,0},{128,64},{192,128},{256,192},{320,256},{384,320},{448,384},... | collective-permute-start | bytes 98312 | tf_op jit(solution)/shard_map/ppermute | solution.py:341
  285.8 2.8 copy-start.3
  285.8 2.8 copy-start.4
  288.6 1.0 copy-start

commit v4 on v3

--- a/solution.py
+++ b/solution.py
@@ -103,7 +103,16 @@
             jnp.full((BLK, weight.shape[1]), ids[block], jnp.int32) >= 0, 0.5, 1.0
         )
     weighted = weight[RIM:, :] * rhs[RIM:, :].astype(F32)
-    sums[...] = narrow_dot(basis[...], weighted, 3)
+    total = narrow_dot(basis[...], weighted, 3)
+    rigid = narrow_dot(global_basis[...], weighted, 3)
+    pad = jnp.zeros((2 * CHUNK - MODES, rigid.shape[1]), F32)
+    rigid = jnp.concatenate([rigid, pad], axis=0)
+    tiles = total.reshape(sums.shape[0], 2 * CHUNK, sums.shape[2])
+    turned = pltpu.roll(rigid, CHUNK, 0)[None]
+    first = lax.broadcasted_iota(jnp.int32, tiles.shape, 1) < CHUNK
+    sums[:, : 2 * CHUNK, :] = jnp.where(first, tiles, turned)
+    sums[:, 2 * CHUNK : 4 * CHUNK, :] = jnp.where(first, turned, tiles)
+    sums[:, 4 * CHUNK :, :] = jnp.broadcast_to(rigid[None], tiles.shape)
     spread_t = one_hot((kc, rows), lambda i, j: j == i + i // (CHUNK - 1))
     solve[...] = wide_dot(wide_dot(spread, inverse[...]), spread_t)
     pick = one_hot(
@@ -128,6 +137,19 @@
         copies[...] = jnp.broadcast_to(
             total[None], (copies.shape[0] // tile, tile, lanes)
         ).reshape(copies.shape)
+
+
+def first_sum_kernel(parts, copies, extra):
+    rows, lanes = copies.shape
+    tile = 2 * CHUNK
+    total = jnp.sum(parts[...], axis=0)
+    even, odd, rigid = total[:tile], total[tile : 2 * tile], total[2 * tile :]
+    first = lax.broadcasted_iota(jnp.int32, even.shape, 0) < CHUNK
+    chunk = jnp.where(first, even, odd)
+    chunk = chunk + pltpu.roll(chunk, CHUNK, 0)
+    copies[...] = jnp.broadcast_to(chunk[None], (rows // tile, tile, lanes)).reshape(rows, lanes)
+    extra[:tile, :] = rigid + pltpu.roll(jnp.where(first, odd, even), CHUNK, 0)
+    extra[tile:, :] = jnp.zeros((EXTRA - tile, lanes), F32)
 
 
 def far_sum_kernel(parts, copies):
@@ -316,12 +338,11 @@
     blocks = ((subs, BLK, lanes), F32)
 
     def reduce_first(sums):
-        (copies,) = call(chunk_sum_kernel, [sums_out], [exchange(sums)], smem=False)
-        projection = exchange(copies)
-        extra = lax.slice(
-            projection, (CHUNK - 1, 0), (slot_row(EXTRA - 1) + 1, lanes), (CHUNK, 1)
+        parts = exchange(sums.reshape(3 * subs, CHUNK, lanes)).reshape(sums.shape)
+        copies, extra = call(
+            first_sum_kernel, [sums_out, ((EXTRA, lanes), F32)], [parts], smem=False
         )
-        return projection, lax.all_gather(extra, "clus", axis=0, tiled=True)
+        return exchange(copies), lax.all_gather(extra, "clus", axis=0, tiled=True)
 
     def reduce_beside(sums):
         (copies,) = call(far_sum_kernel, [sums_out], [exchange_far(sums)], smem=False)
@@ -343,7 +364,7 @@
 
     sums, basis, basis_t, weight, solve, global_solve = call(
         prepare_kernel,
-        [sums_out, ((n, cluster_basis.shape[2]), BF16), ((cluster_basis.shape[2], n), BF16), vector, ((n, n), F32),
+        [((subs // 2, 6 * CHUNK, lanes), F32), ((n, cluster_basis.shape[2]), BF16), ((cluster_basis.shape[2], n), BF16), vector, ((n, n), F32),
          ((n, clusters * EXTRA), F32)],
         [ids, rhs, cluster_basis[0], global_basis[0], cluster_inverse[0], global_inverse],
     )

time: 350 us -> 354 us (1.011)
  starting transfers between devices: 28.7 us -> 38.2 us
  blocking collectives: 266 us -> 260 us
    all_to_all x3 -> x2, blocking collectives: 86.7 us -> 75.7 us  [exchange(): lax.all_to_all(values, 'sub', split_axis=0, concat_axis=0, tiled=True)]
    all_to_all x2 -> x3, starting transfers between devices: 14.6 us -> 23.7 us  [exchange(): lax.all_to_all(values, 'sub', split_axis=0, concat_axis=0, tiled=True)]
    all_to_all x4, blocking collectives: 69.3 us -> 76.3 us  [exchange_far(): lax.all_to_all(values, 'sub', split_axis=0, concat_axis=0, tiled=True, ax...]
    all_to_all x2 -> x3, waiting for transfers between devices: 14.2 us -> 13.3 us  [exchange(): lax.all_to_all(values, 'sub', split_axis=0, concat_axis=0, tiled=True)]
  transfers between devices with their start and end apart: 6 -> 7, of which waited for: 2 -> 2; matrix products, arithmetic and copies ran while one was open for 0% -> 0% of each run, Pallas kernels for 1% -> 1%
where the time goes in v4:
time: 354 us; the launch traced here: 353 us
  blocking collectives  260 us (73%)
  starting transfers between devices  38.2 us (11%)
  Pallas kernels  37.1 us (10%)
  waiting for transfers between devices  13.3 us (4%)
    all_to_all x4, blocking collectives, exchange_far(): lax.all_to_all(values, 'sub', split_axis=0, concat_axis=0, tiled=True, ax...  76.3 us
    all_to_all x2, blocking collectives, exchange(): lax.all_to_all(values, 'sub', split_axis=0, concat_axis=0, tiled=True)  75.7 us
    all_gather x2, blocking collectives, reduce_beside(): return (projection, lax.all_gather(extra, 'clus', axis=0, tiled=True))  39.2 us
    pallas_call x11, Pallas kernels, call(): pl.pallas_call(kernel, out_shape=[jax.ShapeDtypeStruct(shape, dtype) for...  37.1 us
    all_gather x2, blocking collectives, reduce_beside(): lax.all_gather(column, 'sub', axis=0, tiled=True, axis_index_groups=near_...  27.1 us
    all_to_all x3, starting transfers between devices, exchange(): lax.all_to_all(values, 'sub', split_axis=0, concat_axis=0, tiled=True)  23.7 us
    all_gather x1, blocking collectives, reduce_first(): return (exchange(copies), lax.all_gather(extra, 'clus', axis=0, tiled=True))  21 us
    all_gather x1, blocking collectives, on_device(): gathered_c = lax.all_gather(total, 'clus', axis=0, tiled=True)  20.8 us
  transfers between devices with their start and end apart: 7, of which 2 were waited for; matrix products, arithmetic and copies ran while one was open for 0% of the time, Pallas kernels for 1%

profile of v4, /device:TPU:1, one launch (start us, length us, event | category | flops | bytes accessed | tf_op | source)
XLA Modules:
  0.0 352.9 jit_solution(12908558259905910757)
XLA Ops:
  0.0 0.7 bitcast_select_fusion.1
  0.7 0.6 pad_add_fusion.ids
  1.3 4.0 %shard_map.73 = (f32[32,24,128]{2,1,0:T(8,128)}, bf16[256,896]{1,0:T(8,128)(2,1)}, bf16[896,256]{1,0:T(8,128)(2,1)}, f32[1024,128]{1,0:T(8,128)}, f32[256,256]{1,0:T(8,128)}, /*index=5*/f32[256,256]{1,0:T(8,128)}) custom-call(s32[32]{0:T(128)} %pad_add_fusion.ids, bf16[1024,128]{1,0:T(8,128)(2,1)} %bitcast.34, bf16[192,896]{1,0:T(8,128)(2,1)} %bitcast.48, ...), custom_call_target="tpu_custom_call" | custom-call | tf_op jit(solution)/shard_map/pallas_call | solution.py:292
  5.3 47.8 %all_to_all.83 = f32[192,4,128]{2,1,0:T(4,128)} all-to-all(f32[192,4,128]{2,1,0:T(4,128)} %bitcast.47), channel_id=1, replica_groups=mesh['clus'=16,'sub'=64] {'sub'}, dimensions={0} | all-to-all | bytes 786432 | tf_op jit(solution)/shard_map/all_to_all | solution.py:318
  53.1 1.7 shard_map.74
  54.8 7.5 %all-to-all-start.1 = ((f32[64,4,128]{2,1,0:T(4,128)}), f32[64,4,128]{2,1,0:T(4,128)S(1)}, u32[]{:S(2)}, u32[]{:S(2)}) async-start(f32[64,4,128]{2,1,0:T(4,128)} %bitcast.52), calls=%async_computation.1 | async-start | bytes 262144 | tf_op jit(solution)/shard_map/all_to_all | solution.py:318
  62.3 21.0 %all_gather.18.gathered = f32[256,128]{1,0:T(8,128)} all-gather(f32[16,128]{1,0:T(8,128)} %get-tuple-element.46), channel_id=1, replica_groups=mesh['clus'=16,'sub'=64] {'clus'}, dimensions={0}, use_global_device_ids=true | all-gather | bytes 139264 | tf_op jit(solution)/shard_map/all_gather | solution.py:345
  83.3 0.0 all-to-all-done.1
  83.3 0.0 copy-start.2
  83.3 0.7 copy-done.2
  84.0 6.4 %shard_map.75 = (f32[1024,128]{1,0:T(8,128)}, f32[1024,128]{1,0:T(8,128)}, f32[256,128]{1,0:T(8,128)}, f32[64,32,128]{2,1,0:T(8,128)}, f32[64,128]{1,0:T(8,128)}, /*index=5*/f32[64,128]{1,0:T(8,128)}) custom-call(s32[32]{0:T(128)} %pad_add_fusion.ids, bf16[1024,128]{1,0:T(8,128)(2,1)} %bitcast.35, bf16[1024,1024]{1,0:T(8,128)(2,1)} %bitcast.31, ...), custom_call_target="tpu_custom_call" | custom-call | tf_op jit(solution)/shard_map/pallas_call | solution.py:292
  90.3 0.0 copy-start.10
  90.3 0.0 copy-start.9
  90.3 23.8 %all_to_all.84 = f32[16,16,128]{2,1,0:T(8,128)} all-to-all(f32[16,16,128]{2,1,0:T(8,128)} %bitcast.53), channel_id=1, replica_groups={{0,4,8,12,16,20,24,28,32,36,40,44,48,52,56,60},{1,5,9,13,17,21,25,29,33..., dimensions={0} | all-to-all | bytes 262144 | tf_op jit(solution)/shard_map/all_to_all | solution.py:312
  114.2 1.6 shard_map.76
  115.8 18.5 %all_to_all.85 = f32[16,16,128]{2,1,0:T(8,128)S(1)} all-to-all(f32[16,16,128]{2,1,0:T(8,128)} %bitcast.43), channel_id=1, replica_groups={{0,4,8,12,16,20,24,28,32,36,40,44,48,52,56,60},{1,5,9,13,17,21,25,29,33..., dimensions={0} | all-to-all | bytes 262144 | tf_op jit(solution)/shard_map/all_to_all | solution.py:312
  134.3 9.3 %all-to-all-start.2 = ((f32[64,32,128]{2,1,0:T(8,128)}), f32[64,32,128]{2,1,0:T(8,128)S(1)}, u32[]{:S(2)}, u32[]{:S(2)}) async-start(f32[64,32,128]{2,1,0:T(8,128)} %get-tuple-element.49), calls=%async_computation.2 | async-start | bytes 2097152 | tf_op jit(solution)/shard_map/all_to_all | solution.py:318
  143.6 0.0 copy-done.10
  143.6 3.1 collective-permute-start
  146.7 0.0 copy-done.9
  146.7 1.9 collective-permute-start.1
  148.7 13.3 %all_gather.19.parts = f32[1024,128]{1,0:T(8,128)} all-gather(f32[256,128]{1,0:T(8,128)S(1)} %bitcast.40), channel_id=1, replica_groups={{0,1,2,3},{4,5,6,7},{8,9,10,11},{12,13,14,15},{16,17,18,19},{20,21,22,2..., dimensions={0}, use_global_device_ids=true | all-gather | bytes 655360 | tf_op jit(solution)/shard_map/all_gather | solution.py:350
  162.0 1.7 shard_map.77
  163.7 20.1 %all_gather.20.gathered_a.gathered_old = f32[256,128]{1,0:T(8,128)} all-gather(f32[16,128]{1,0:T(8,128)} %get-tuple-element.54), channel_id=1, replica_groups=mesh['clus'=16,'sub'=64] {'clus'}, dimensions={0}, use_global_device_ids=true | all-gather | bytes 139264 | tf_op jit(solution)/shard_map/all_gather | solution.py:356
  183.8 0.0 collective-permute-done.from_low
  183.8 0.0 copy-start.5
  183.8 0.0 collective-permute-done.1.from_high
  183.8 0.0 copy-start.6
  183.9 10.9 %all-to-all-done.2.incoming = f32[64,32,128]{2,1,0:T(8,128)S(1)} async-done(((f32[64,32,128]{2,1,0:T(8,128)}), f32[64,32,128]{2,1,0:T(8,128)S(1)}, u32[]{:S(2)}, u32[]{:S(2)}) %all-to-all-start.2) | async-done | bytes 1048608 | tf_op jit(solution)/shard_map/all_to_all | solution.py:318
  194.8 0.0 copy-start.1
  194.8 0.0 copy-done.5
  194.8 0.0 copy-done.6
  194.8 0.9 copy-done.1
  195.7 7.5 %shard_map.78 = (f32[1024,128]{1,0:T(8,128)}, f32[1024,128]{1,0:T(8,128)}, f32[256,128]{1,0:T(8,128)}, f32[256,128]{1,0:T(8,128)}, f32[8,128]{1,0:T(8,128)}, /*i...) custom-call(s32[32]{0:T(128)} %pad_add_fusion.ids, ...), custom_call_target="tpu_custom_call" | custom-call | tf_op jit(solution)/shard_map/pallas_call | solution.py:292
  203.2 0.0 copy-start.8
  203.3 0.0 copy-start.7
  203.3 18.0 %all_to_all.86 = f32[16,16,128]{2,1,0:T(8,128)} all-to-all(f32[16,16,128]{2,1,0:T(8,128)} %bitcast.51), channel_id=1, replica_groups={{0,4,8,12,16,20,24,28,32,36,40,44,48,52,56,60},{1,5,9,13,17,21,25,29,33..., dimensions={0} | all-to-all | bytes 262144 | tf_op jit(solution)/shard_map/all_to_all | solution.py:312
  221.3 1.6 shard_map.79
  222.8 16.0 %all_to_all.87 = f32[16,16,128]{2,1,0:T(8,128)S(1)} all-to-all(f32[16,16,128]{2,1,0:T(8,128)} %bitcast.45), channel_id=1, replica_groups={{0,4,8,12,16,20,24,28,32,36,40,44,48,52,56,60},{1,5,9,13,17,21,25,29,33..., dimensions={0} | all-to-all | bytes 262144 | tf_op jit(solution)/shard_map/all_to_all | solution.py:312
  238.8 6.9 %all-to-all-start.5 = ((f32[64,32,128]{2,1,0:T(8,128)}), f32[64,32,128]{2,1,0:T(8,128)S(1)}, u32[]{:S(2)}, u32[]{:S(2)}) async-start(f32[64,32,128]{2,1,0:T(8,128)} %get-tuple-element.62), calls=%async_computation.5 | async-start | bytes 2097152 | tf_op jit(solution)/shard_map/all_to_all | solution.py:318
  245.8 0.0 copy-done.8
  245.8 7.5 %collective-permute-start.2 = (f32[64,128]{1,0:T(8,128)S(1)}, f32[64,128]{1,0:T(8,128)S(1)}, u32[]{:S(2)}, u32[]{:S(2)}) collective-permute-start(f32[64,128]{1,0:T(8,128)S(1)} %copy-done.8), channel_id=1, source_target_pairs={{0,64},{64,128},{128,192},{192,256},{256,320},{320,384},{384,448},... | collective-permute-start | bytes 98312 | tf_op jit(solution)/shard_map/ppermute | solution.py:361
  253.3 0.0 copy-done.7
  253.3 1.9 collective-permute-start.3
  255.2 13.8 %all_gather.21.parts = f32[1024,128]{1,0:T(8,128)} all-gather(f32[256,128]{1,0:T(8,128)S(1)} %bitcast.41), channel_id=1, replica_groups={{0,1,2,3},{4,5,6,7},{8,9,10,11},{12,13,14,15},{16,17,18,19},{20,21,22,2..., dimensions={0}, use_global_device_ids=true | all-gather | bytes 655360 | tf_op jit(solution)/shard_map/all_gather | solution.py:350
  269.0 1.7 shard_map.80
  270.8 19.1 %all_gather.22.gathered_a = f32[256,128]{1,0:T(8,128)} all-gather(f32[16,128]{1,0:T(8,128)} %get-tuple-element.67), channel_id=1, replica_groups=mesh['clus'=16,'sub'=64] {'clus'}, dimensions={0}, use_global_device_ids=true | all-gather | bytes 139264 | tf_op jit(solution)/shard_map/all_gather | solution.py:356
  289.9 0.0 collective-permute-done.2.from_low
  289.9 0.0 copy-start.3
  289.9 0.0 collective-permute-done.3.from_high
  289.9 0.0 copy-start.4
  289.9 2.3 all-to-all-done.5.incoming
  292.3 0.0 copy-start
  292.3 0.0 copy-done.3
  292.3 0.0 copy-done.4
  292.3 1.0 copy-done
  293.3 7.0 %shard_map.81 = (f32[1024,128]{1,0:T(8,128)}, f32[1024,128]{1,0:T(8,128)}, f32[1024,128]{1,0:T(8,128)}, f32[8,128]{1,0:T(8,128)}, f32[256,128]{1,0:T(8,128)}) custom-call(s32[32]{0:T(128)} %pad_add_fusion.ids, bf16[1024,1024]{1,0:T(8,128)(2,1)} %bitcast.33, bf16[256,896]{1,0:T(8,128)(2,1)} %get-tuple-element.39.basis, ...), custom_call_target="tpu_custom_call" | custom-call | tf_op jit(solution)/shard_map/pallas_call | solution.py:292
  300.3 27.9 %all_to_all.88 = f32[64,4,128]{2,1,0:T(4,128)} all-to-all(f32[64,4,128]{2,1,0:T(4,128)} %bitcast.50), channel_id=1, replica_groups=mesh['clus'=16,'sub'=64] {'sub'}, dimensions={0} | all-to-all | bytes 262144 | tf_op jit(solution)/shard_map/all_to_all | solution.py:318
  328.2 1.5 shard_map.82
  329.8 20.8 %all_gather.23.gathered = f32[128,128]{1,0:T(8,128)} all-gather(f32[8,128]{1,0:T(8,128)} %shard_map.82), channel_id=1, replica_groups=mesh['clus'=16,'sub'=64] {'clus'}, dimensions={0}, use_global_device_ids=true | all-gather | bytes 69632 | tf_op jit(solution)/shard_map/all_gather | solution.py:402
  350.6 2.3 shard_map.83
  (1 shorter events, 0.0 us)
Async XLA Ops:
  54.8 28.5 %all-to-all-start.1 = ((f32[64,4,128]{2,1,0:T(4,128)}), f32[64,4,128]{2,1,0:T(4,128)S(1)}, u32[]{:S(2)}, u32[]{:S(2)}) async-start(f32[64,4,128]{2,1,0:T(4,128)} %bitcast.52), calls=%async_computation.1 | async-start | bytes 262144 | tf_op jit(solution)/shard_map/all_to_all | solution.py:318
  83.3 0.7 copy-start.2
  90.3 53.2 %copy-start.10 = (f32[64,128]{1,0:T(8,128)S(1)}, f32[64,128]{1,0:T(8,128)}, u32[]{:S(2)}) copy-start(f32[64,128]{1,0:T(8,128)} %get-tuple-element.50) | copy-start | bytes 98308
  90.3 56.4 %copy-start.9 = (f32[64,128]{1,0:T(8,128)S(1)}, f32[64,128]{1,0:T(8,128)}, u32[]{:S(2)}) copy-start(f32[64,128]{1,0:T(8,128)} %get-tuple-element.51) | copy-start | bytes 98308
  134.3 60.5 %all-to-all-start.2 = ((f32[64,32,128]{2,1,0:T(8,128)}), f32[64,32,128]{2,1,0:T(8,128)S(1)}, u32[]{:S(2)}, u32[]{:S(2)}) async-start(f32[64,32,128]{2,1,0:T(8,128)} %get-tuple-element.49), calls=%async_computation.2 | async-start | bytes 2097152 | tf_op jit(solution)/shard_map/all_to_all | solution.py:318
  143.6 40.3 %collective-permute-start = (f32[64,128]{1,0:T(8,128)S(1)}, f32[64,128]{1,0:T(8,128)S(1)}, u32[]{:S(2)}, u32[]{:S(2)}) collective-permute-start(f32[64,128]{1,0:T(8,128)S(1)} %copy-done.10), channel_id=1, source_target_pairs={{0,64},{64,128},{128,192},{192,256},{256,320},{320,384},{384,448},... | collective-permute-start | bytes 98312 | tf_op jit(solution)/shard_map/ppermute | solution.py:361
  146.7 37.1 %collective-permute-start.1 = (f32[64,128]{1,0:T(8,128)S(1)}, f32[64,128]{1,0:T(8,128)S(1)}, u32[]{:S(2)}, u32[]{:S(2)}) collective-permute-start(f32[64,128]{1,0:T(8,128)S(1)} %copy-done.9), channel_id=1, source_target_pairs={{64,0},{128,64},{192,128},{256,192},{320,256},{384,320},{448,384},... | collective-permute-start | bytes 98312 | tf_op jit(solution)/shard_map/ppermute | solution.py:362
  183.8 10.9 %copy-start.5 = (f32[64,128]{1,0:T(8,128)}, f32[64,128]{1,0:T(8,128)S(1)}, u32[]{:S(2)}) copy-start(f32[64,128]{1,0:T(8,128)S(1)} %collective-permute-done.from_low) | copy-start | bytes 98308
  183.8 10.9 %copy-start.6 = (f32[64,128]{1,0:T(8,128)}, f32[64,128]{1,0:T(8,128)S(1)}, u32[]{:S(2)}) copy-start(f32[64,128]{1,0:T(8,128)S(1)} %collective-permute-done.1.from_high) | copy-start | bytes 98308
  194.8 0.9 copy-start.1
  203.2 42.5 %copy-start.8 = (f32[64,128]{1,0:T(8,128)S(1)}, f32[64,128]{1,0:T(8,128)}, u32[]{:S(2)}) copy-start(f32[64,128]{1,0:T(8,128)} %get-tuple-element.63) | copy-start | bytes 98308
  203.3 50.0 %copy-start.7 = (f32[64,128]{1,0:T(8,128)S(1)}, f32[64,128]{1,0:T(8,128)}, u32[]{:S(2)}) copy-start(f32[64,128]{1,0:T(8,128)} %get-tuple-element.64) | copy-start | bytes 98308
  238.8 53.4 %all-to-all-start.5 = ((f32[64,32,128]{2,1,0:T(8,128)}), f32[64,32,128]{2,1,0:T(8,128)S(1)}, u32[]{:S(2)}, u32[]{:S(2)}) async-start(f32[64,32,128]{2,1,0:T(8,128)} %get-tuple-element.62), calls=%async_computation.5 | async-start | bytes 2097152 | tf_op jit(solution)/shard_map/all_to_all | solution.py:318
  245.8 44.1 %collective-permute-start.2 = (f32[64,128]{1,0:T(8,128)S(1)}, f32[64,128]{1,0:T(8,128)S(1)}, u32[]{:S(2)}, u32[]{:S(2)}) collective-permute-start(f32[64,128]{1,0:T(8,128)S(1)} %copy-done.8), channel_id=1, source_target_pairs={{0,64},{64,128},{128,192},{192,256},{256,320},{320,384},{384,448},... | collective-permute-start | bytes 98312 | tf_op jit(solution)/shard_map/ppermute | solution.py:361
  253.3 36.6 %collective-permute-start.3 = (f32[64,128]{1,0:T(8,128)S(1)}, f32[64,128]{1,0:T(8,128)S(1)}, u32[]{:S(2)}, u32[]{:S(2)}) collective-permute-start(f32[64,128]{1,0:T(8,128)S(1)} %copy-done.7), channel_id=1, source_target_pairs={{64,0},{128,64},{192,128},{256,192},{320,256},{384,320},{448,384},... | collective-permute-start | bytes 98312 | tf_op jit(solution)/shard_map/ppermute | solution.py:362
  289.9 2.4 copy-start.3
  289.9 2.4 copy-start.4
  292.3 1.0 copy-start
